TPU v7x, 128 devices: a whole 4x4x4 slice. The times are simulated.
128 devices in a mesh: leaf: 32 (over x, z, core), level: 4 (over y).
Axes of the slice: x: 4, y: 4, z: 4, core: 2. Of those that a mesh axis runs over, the one named last changes fastest.
Arguments:
- right_side: float32 [8, 2097152], P(None, ('leaf', 'level')), may hold values from -28 to 28
- basis: bfloat16 [16384, 128, 128], P(('leaf', 'level')), may hold values from -0.5 to 0.5
- transfer: bfloat16 [16384, 128, 128], P(('leaf', 'level')), may hold values from -0.5 to 0.5
- order: int32 [128, 128], P(('leaf', 'level')), may hold values from 0 to 127, each once within a row
- far_src: int32 [4096, 4], P(('leaf', 'level')), may hold values from 0 to 127
- far_mats: bfloat16 [4096, 4, 128, 128], P(('leaf', 'level')), may hold values from -0.125 to 0.125
- near_target: int32 [32768], P(('leaf', 'level')), may hold values from 0 to 127
- near_dest: int32 [32768, 1], P(('leaf', 'level')), may hold values from 0 to 127; in each aligned block of 256 rows (0 to 255, 256 to 511, ...) at most 4 rows name the same one
- near_src: int32 [32768], P(('leaf', 'level')), may hold values from 0 to 127
- near_blocks: bfloat16 [32768, 128, 128], P(('leaf', 'level')), may hold values from -0.5 to 0.5
Outputs:
- solution: float32 [8, 2097152], P(None, ('leaf', 'level'))
- residual: float32 [8, 2097152], P(None, ('leaf', 'level'))
Inputs may be any that keep to these rules, and one draw needn't show every extreme that they name: `order`: each group's row is a permutation of 0 to 127. `near_dest`: among the pairs of one group, no group is named more than 4 times, a bound that some block reaches.
All inputs are finite; a program needn't handle non-finite values.
Results may differ from a plain program's by a relative error of at most 0.0022.
Values may be sent and summed in bfloat16 or wider, within the bound.
A program may use at most 128 MiB of HBM per device.

v0:
```python
import jax
import jax.numpy as jnp
from jax import lax
from jax.sharding import PartitionSpec as P

CHILDREN = 4


EPSILON = 1e-06


def local(
    right_side,
    basis,
    transfer,
    order,
    far_src,
    far_mats,
    near_target,
    near_dest,
    near_src,
    near_blocks,
):
    systems = right_side.shape[0]
    clusters, points, coeffs = basis.shape
    groups = lax.axis_size(("leaf", "level"))
    capacity = max(4, 2 * near_dest.shape[0] // groups)
    parents = clusters // CHILDREN
    partners = far_src.shape[1]
    permutation = order[0]
    positions = jnp.arange(clusters, dtype=jnp.int32)
    inverse = jnp.zeros((clusters,), jnp.int32).at[permutation].set(positions)
    basis_slot = jnp.take(basis, permutation, axis=0)
    transfer_slot = jnp.take(transfer, permutation, axis=0)
    targets = near_dest[:, 0]
    member = (targets[:, None] == jnp.arange(groups, dtype=jnp.int32)[None, :]).astype(jnp.int32)
    slot_rank = jnp.sum(jnp.cumsum(member, axis=0) * member, axis=1) - 1
    slot_index = targets * capacity + slot_rank
    source_label = (
        jnp.full((groups * capacity,), -1.0, jnp.float32)
        .at[slot_index]
        .set(near_src.astype(jnp.float32))
    )
    cluster_ids = positions.astype(jnp.float32)

    def near_field(rounded):
        columns = jnp.take(rounded, near_target, axis=1)
        partial_rows = jnp.einsum(
            "rnp,npq->nrq", columns, near_blocks, preferred_element_type=jnp.float32
        )
        outgoing = (
            jnp.zeros((groups * capacity, systems, points), jnp.float32)
            .at[slot_index]
            .set(partial_rows)
        )
        incoming, labels = (
            lax.all_to_all(
                outgoing.astype(jnp.bfloat16),
                ("leaf", "level"),
                split_axis=0,
                concat_axis=0,
                tiled=True,
            ).astype(outgoing.dtype),
            lax.all_to_all(
                source_label.astype(jnp.bfloat16),
                ("leaf", "level"),
                split_axis=0,
                concat_axis=0,
                tiled=True,
            ).astype(source_label.dtype),
        )
        landing = (labels[:, None] == cluster_ids[None, :]).astype(jnp.float32)
        return jnp.einsum("sc,srp->rcp", landing, incoming, precision=lax.Precision.HIGHEST)

    def upward(lifted):
        arrived = lax.all_to_all(lifted, ("leaf", "level"), split_axis=0, concat_axis=0, tiled=True)
        return arrived

    def downward(spread):
        returned = lax.all_to_all(
            spread, ("leaf", "level"), split_axis=0, concat_axis=0, tiled=True
        )
        return returned

    def operator(vector_in):
        rounded = vector_in.astype(jnp.bfloat16).reshape(systems, clusters, points)
        near_sum = near_field(rounded)
        ordered = jnp.take(rounded, permutation, axis=1)
        expansion = jnp.einsum(
            "rsp,spk->srk", ordered, basis_slot, preferred_element_type=jnp.float32
        ).astype(jnp.bfloat16)
        lifted = jnp.einsum(
            "srk,skj->srj", expansion, transfer_slot, preferred_element_type=jnp.float32
        )
        arrived = upward(lifted)
        parent_rows = jnp.sum(arrived.reshape(parents, CHILDREN, systems, coeffs), axis=1).astype(
            jnp.bfloat16
        )
        parent_table = lax.all_gather(parent_rows, "level", axis=0, tiled=True)
        picked = jnp.take(parent_table, far_src.reshape(-1), axis=0).reshape(
            parents, partners, systems, coeffs
        )
        translated = jnp.einsum(
            "qfrk,qfkj->qrj", picked, far_mats, preferred_element_type=jnp.float32
        ).astype(jnp.bfloat16)
        returned = downward(jnp.repeat(translated, CHILDREN, axis=0))
        expanded = jnp.einsum(
            "srk,sjk->srj", returned, transfer_slot, preferred_element_type=jnp.float32
        ).astype(jnp.bfloat16)
        far_slot = jnp.einsum(
            "srk,spk->rsp", expanded, basis_slot, preferred_element_type=jnp.float32
        )
        far_sum = jnp.take(far_slot, inverse, axis=1)
        total = 0.5 * vector_in.reshape(systems, clusters, points) + near_sum + far_sum
        return total.reshape(systems, clusters * points)

    sq_start = lax.psum(jnp.sum(right_side * right_side, axis=1), ("leaf", "level"))
    start_norm = jnp.sqrt(sq_start + EPSILON)
    basis_one = right_side / start_norm[:, None]
    image_one = operator(basis_one)
    along_one = lax.psum(jnp.sum(basis_one * image_one, axis=1), ("leaf", "level"))
    remain = image_one - along_one[:, None] * basis_one
    rest_sq = lax.psum(jnp.sum(remain * remain, axis=1), ("leaf", "level"))
    rest_one = jnp.sqrt(rest_sq + EPSILON)
    basis_two = remain / rest_one[:, None]
    image_two = operator(basis_two)
    cross_two, along_two = lax.psum(
        (jnp.sum(basis_one * image_two, axis=1), jnp.sum(basis_two * image_two, axis=1)),
        ("leaf", "level"),
    )
    leftover = image_two - cross_two[:, None] * basis_one - along_two[:, None] * basis_two
    tail_sq = lax.psum(jnp.sum(leftover * leftover, axis=1), ("leaf", "level"))
    gram_first = along_one * along_one + rest_one * rest_one
    gram_cross = along_one * cross_two + rest_one * along_two
    gram_last = cross_two * cross_two + along_two * along_two + tail_sq
    determinant = gram_first * gram_last - gram_cross * gram_cross
    coef_one = start_norm * (along_one * gram_last - cross_two * gram_cross) / determinant
    coef_two = start_norm * (gram_first * cross_two - gram_cross * along_one) / determinant
    solution = coef_one[:, None] * basis_one + coef_two[:, None] * basis_two
    residual = right_side - coef_one[:, None] * image_one - coef_two[:, None] * image_two
    return (solution, residual)


def solution(mesh):
    placed = (
        P(None, ("leaf", "level")),
        P(("leaf", "level"), None, None),
        P(("leaf", "level"), None, None),
        P(("leaf", "level"), None),
        P(("leaf", "level"), None),
        P(("leaf", "level"), None, None, None),
        P(("leaf", "level")),
        P(("leaf", "level"), None),
        P(("leaf", "level")),
        P(("leaf", "level"), None, None),
    )
    return jax.shard_map(
        local,
        mesh=mesh,
        in_specs=placed,
        out_specs=(P(None, ("leaf", "level")), P(None, ("leaf", "level"))),
        check_vma=False,
    )
```

profile of v0, /device:TPU:1, one launch (start us, length us, event | category | flops | bytes accessed | tf_op | source)
XLA Modules:
  0.0 548.3 jit_solution(14500111837236698376)
XLA Ops:
  3.2 68.6 %psum.42 = f32[8]{0:T(128)S(1)} all-reduce(f32[8]{0:T(128)S(1)} %multiply_reduce_fusion.1), channel_id=1, replica_groups=mesh['leaf'=32,'level'=4] {'leaf','level'}, use_global_device_ids=true, to_apply=%region_1.2 | all-reduce | flops 8 | bytes 64 | tf_op jit(solution)/shard_map/psum | solution.py:117
  74.6 5.2 gather_fusion.3
  85.0 6.7 %fusion.4 = f32[128,8,128]{2,1,0:T(8,128)} fusion(bf16[128,8,128]{2,1,0:T(8,128)(2,1)S(1)} %gather_fusion.2, pred[128]{0:T(512)(128)(4,1)S(1)} %compare_and_fusion.2, bf16[128,128,128]{2,1,0:T(8,128)(2,1)} %gather_fusion.1, bf16[128,128,128]{2,1,0:T(8,128)(2,1)} %gather_fusion.3), kind=kOutput, calls=%fused_computation.28 | convolution fusion | flops 71565312 | bytes 9175168 | tf_op jit(solution)/shard_map/srk,skj->srj/dot_general | solution.py:92
  91.7 5.4 all-to-all-start.2
  105.9 7.0 %scatter_fusion = f32[512,8,128]{2,1,0:T(8,128)S(1)} fusion(f32[512,8,128]{2,1,0:T(8,128)S(1)} %broadcast.90.clone, s32[256]{0:T(256)S(1)} %bitcast.157, f32[256,8,128]{2,1,0:T(8,128)S(1)} %fusion.20), kind=kCustom, calls=%fused_computation.10 | custom fusion | bytes 3146752 | tf_op jit(solution)/shard_map/scatter | solution.py:54
  115.1 9.9 %all-to-all-start.1 = ((bf16[128,4,1]{1,2,0:T(2,128)(2,1)}), bf16[128,4,1]{1,2,0:T(2,128)(2,1)S(1)}, u32[]{:S(2)}, u32[]{:S(2)}) async-start(bf16[128,4,1]{1,2,0:T(2,128)(2,1)} %all_to_all.33), calls=%async_computation.1 | async-start | bytes 131072 | tf_op jit(solution)/shard_map/all_to_all | solution.py:64
  126.1 10.6 %all_gather.6 = bf16[128,8,128]{2,1,0:T(8,128)(2,1)S(1)} all-gather(bf16[32,8,128]{2,1,0:T(8,128)(2,1)S(1)} %bitcast_reduce_fusion.1), channel_id=1, replica_groups=mesh['leaf'=32,'level'=4] {'level'}, dimensions={0}, use_global_device_ids=true | all-gather | bytes 327680 | tf_op jit(solution)/shard_map/all_gather | solution.py:99
  141.2 11.4 %all-to-all-start.3 = ((bf16[128,8,128]{2,1,0:T(8,128)(2,1)}), bf16[128,8,128]{2,1,0:T(8,128)(2,1)S(1)}, u32[]{:S(2)}, u32[]{:S(2)}) async-start(bf16[128,8,128]{2,1,0:T(8,128)(2,1)} %bitcast.19), calls=%async_computation.3 | async-start | bytes 524288 | tf_op jit(solution)/shard_map/all_to_all | solution.py:80
  152.7 11.3 %all-to-all-done.3 = bf16[128,8,128]{2,1,0:T(8,128)(2,1)S(1)} async-done(((bf16[128,8,128]{2,1,0:T(8,128)(2,1)}), bf16[128,8,128]{2,1,0:T(8,128)(2,1)S(1)}, u32[]{:S(2)}, u32[]{:S(2)}) %all-to-all-start.3) | async-done | bytes 262176 | tf_op jit(solution)/shard_map/all_to_all | solution.py:80
  168.5 6.9 %convolution_bitcast_fusion.1 = f32[8,128,128]{2,0,1:T(8,128)S(1)} fusion(bf16[128,8,128]{2,1,0:T(8,128)(2,1)S(1)} %all-to-all-done.3, bf16[128,128,128]{2,1,0:T(8,128)(2,1)} %gather_fusion.1, pred[128]{0:T(512)(128)(4,1)S(1)} %compare_and_fusion.2, bf16[128,128,128]{2,1,0:T(8,128)(2,1)} %gather_fusion.3), kind=kOutput, calls=%fused_computation.17 | convolution fusion | flops 71434240 | bytes 9175168 | tf_op jit(solution)/shard_map/srk,spk->rsp/dot_general | solution.py:110
  176.4 11.3 %all-to-all-done = bf16[512,8,128]{2,1,0:T(8,128)(2,1)S(1)} async-done(((bf16[512,8,128]{2,1,0:T(8,128)(2,1)}), bf16[512,8,128]{2,1,0:T(8,128)(2,1)S(1)}, u32[]{:S(2)}, u32[]{:S(2)}) %all-to-all-start) | async-done | bytes 1048608 | tf_op jit(solution)/shard_map/all_to_all | solution.py:57
  188.9 62.7 %psum.43 = f32[8]{0:T(128)S(1)} all-reduce(f32[8]{0:T(128)S(1)} %fusion.16), channel_id=1, replica_groups=mesh['leaf'=32,'level'=4] {'leaf','level'}, use_global_device_ids=true, to_apply=%region_10.16 | all-reduce | flops 8 | bytes 64 | tf_op jit(solution)/shard_map/psum | solution.py:121
  252.0 62.7 %psum.44 = f32[8]{0:T(128)S(1)} all-reduce(f32[8]{0:T(128)S(1)} %multiply_reduce_fusion), channel_id=1, replica_groups=mesh['leaf'=32,'level'=4] {'leaf','level'}, use_global_device_ids=true, to_apply=%region_12.18 | all-reduce | flops 8 | bytes 64 | tf_op jit(solution)/shard_map/psum | solution.py:123
  316.5 6.6 %fusion.5 = f32[128,8,128]{2,1,0:T(8,128)} fusion(bf16[128,8,128]{2,1,0:T(8,128)(2,1)S(1)} %gather_fusion.7, pred[128]{0:T(512)(128)(4,1)S(1)} %compare_and_fusion.2, bf16[128,128,128]{2,1,0:T(8,128)(2,1)} %gather_fusion.1, bf16[128,128,128]{2,1,0:T(8,128)(2,1)} %gather_fusion.3), kind=kOutput, calls=%fused_computation.29 | convolution fusion | flops 71565312 | bytes 9175168 | tf_op jit(solution)/shard_map/srk,skj->srj/dot_general | solution.py:92
  329.2 13.3 %all-to-all-done.5 = f32[128,8,128]{2,1,0:T(8,128)S(1)} async-done(((f32[128,8,128]{2,1,0:T(8,128)}), f32[128,8,128]{2,1,0:T(8,128)S(1)}, u32[]{:S(2)}, u32[]{:S(2)}) %all-to-all-start.5) | async-done | bytes 524320 | tf_op jit(solution)/shard_map/all_to_all | solution.py:76
  342.5 9.4 %all_gather.7 = bf16[128,8,128]{2,1,0:T(8,128)(2,1)S(1)} all-gather(bf16[32,8,128]{2,1,0:T(8,128)(2,1)S(1)} %bitcast_reduce_fusion), channel_id=1, replica_groups=mesh['leaf'=32,'level'=4] {'level'}, dimensions={0}, use_global_device_ids=true | all-gather | bytes 327680 | tf_op jit(solution)/shard_map/all_gather | solution.py:99
  356.4 7.6 %all-to-all-start.6 = ((bf16[128,8,128]{2,1,0:T(8,128)(2,1)}), bf16[128,8,128]{2,1,0:T(8,128)(2,1)S(1)}, u32[]{:S(2)}, u32[]{:S(2)}) async-start(bf16[128,8,128]{2,1,0:T(8,128)(2,1)} %bitcast.30), calls=%async_computation.6 | async-start | bytes 524288 | tf_op jit(solution)/shard_map/all_to_all | solution.py:80
  364.0 6.8 %fusion.18 = f32[256,8,128]{2,1,0:T(8,128)} fusion(bf16[256,128,128]{2,1,0:T(8,128)(2,1)} %param.29, bf16[256,8,128]{2,1,0:T(8,128)(2,1)S(1)} %gather_fusion.6, pred[256]{0:T(512)(128)(4,1)S(1)} %compare_and_fusion.3), kind=kOutput, calls=%fused_computation.54 | convolution fusion | flops 67371008 | bytes 9961728 | tf_op jit(solution)/shard_map/rnp,npq->nrq/dot_general | solution.py:48
  370.9 16.7 %scatter_fusion.1 = f32[512,8,128]{2,1,0:T(8,128)S(1)} fusion(f32[512,8,128]{2,1,0:T(8,128)S(1)} %broadcast.90, s32[256]{0:T(256)S(1)} %bitcast.158, f32[256,8,128]{2,1,0:T(8,128)} %fusion.18), kind=kCustom, calls=%fused_computation.13 | custom fusion | bytes 3146752 | tf_op jit(solution)/shard_map/scatter | solution.py:54
  388.8 9.8 %all-to-all-start.4 = ((bf16[512,8,128]{2,1,0:T(8,128)(2,1)}), bf16[512,8,128]{2,1,0:T(8,128)(2,1)S(1)}, u32[]{:S(2)}, u32[]{:S(2)}) async-start(bf16[512,8,128]{2,1,0:T(8,128)(2,1)} %convert_element_type.83), calls=%async_computation.4 | async-start | bytes 2097152 | tf_op jit(solution)/shard_map/all_to_all | solution.py:57
  400.8 8.8 %convolution_bitcast_fusion = f32[8,128,128]{2,0,1:T(8,128)} fusion(bf16[128,8,128]{2,1,0:T(8,128)(2,1)S(1)} %all-to-all-done.6, bf16[128,128,128]{2,1,0:T(8,128)(2,1)} %gather_fusion.1, pred[128]{0:T(512)(128)(4,1)S(1)} %compare_and_fusion.2, bf16[128,128,128]{2,1,0:T(8,128)(2,1)} %gather_fusion.3), kind=kOutput, calls=%fused_computation.16 | convolution fusion | flops 71434240 | bytes 9175168 | tf_op jit(solution)/shard_map/srk,spk->rsp/dot_general | solution.py:110
  412.3 6.0 %all-to-all-done.4 = bf16[512,8,128]{2,1,0:T(8,128)(2,1)S(1)} async-done(((bf16[512,8,128]{2,1,0:T(8,128)(2,1)}), bf16[512,8,128]{2,1,0:T(8,128)(2,1)S(1)}, u32[]{:S(2)}, u32[]{:S(2)}) %all-to-all-start.4) | async-done | bytes 1048608 | tf_op jit(solution)/shard_map/all_to_all | solution.py:57
  420.9 62.6 %all-reduce = (f32[8]{0:T(128)S(1)}, f32[8]{0:T(128)S(1)}) all-reduce(f32[8]{0:T(128)S(1)} %get-tuple-element.6, f32[8]{0:T(128)S(1)} %get-tuple-element.4), channel_id=1, replica_groups=mesh['leaf'=32,'level'=4] {'leaf','level'}, use_global_device_ids=true, to_apply=%region_16.22 | all-reduce | flops 16 | bytes 128 | tf_op jit(solution)/shard_map/psum | solution.py:127
  484.0 62.7 %psum.47 = f32[8]{0:T(128)S(1)} all-reduce(f32[8]{0:T(128)S(1)} %fusion.14), channel_id=1, replica_groups=mesh['leaf'=32,'level'=4] {'leaf','level'}, use_global_device_ids=true, to_apply=%region_20.26 | all-reduce | flops 8 | bytes 64 | tf_op jit(solution)/shard_map/psum | solution.py:132
  (100 shorter events, 57.2 us)
Async XLA Ops:
  85.0 12.1 %copy-start.7 = (s32[1,128]{1,0:T(1,128)S(1)}, s32[1,128]{1,0:T(1,128)}, u32[]{:S(2)}) copy-start(s32[1,128]{1,0:T(1,128)} %param.23) | copy-start | bytes 1540
  85.0 12.1 %copy-start.5 = (s32[256]{0:T(256)S(1)}, s32[256]{0:T(256)}, u32[]{:S(2)}) copy-start(s32[256]{0:T(256)} %param.26) | copy-start | bytes 3076
  85.0 12.1 %copy-start.6 = (s32[256]{0:T(256)S(1)}, s32[256]{0:T(256)}, u32[]{:S(2)}) copy-start(s32[256]{0:T(256)} %param.28) | copy-start | bytes 3076
  85.0 12.2 %copy-start.4 = (s32[32,4]{0,1:T(4,128)S(1)}, s32[32,4]{0,1:T(4,128)}, u32[]{:S(2)}) copy-start(s32[32,4]{0,1:T(4,128)} %param.24) | copy-start | bytes 1540
  85.0 12.4 %copy-start.3 = (s32[256,1]{0,1:T(1,128)S(1)}, s32[256,1]{0,1:T(1,128)}, u32[]{:S(2)}) copy-start(s32[256,1]{0,1:T(1,128)} %param.27) | copy-start | bytes 3076
  91.7 23.4 %all-to-all-start.2 = ((f32[128,8,128]{2,1,0:T(8,128)}), f32[128,8,128]{2,1,0:T(8,128)}, u32[]{:S(2)}, u32[]{:S(2)}) async-start(f32[128,8,128]{2,1,0:T(8,128)} %fusion.4), calls=%async_computation.2 | async-start | bytes 1048576 | tf_op jit(solution)/shard_map/all_to_all | solution.py:76
  115.1 25.4 %all-to-all-start.1 = ((bf16[128,4,1]{1,2,0:T(2,128)(2,1)}), bf16[128,4,1]{1,2,0:T(2,128)(2,1)S(1)}, u32[]{:S(2)}, u32[]{:S(2)}) async-start(bf16[128,4,1]{1,2,0:T(2,128)(2,1)} %all_to_all.33), calls=%async_computation.1 | async-start | bytes 131072 | tf_op jit(solution)/shard_map/all_to_all | solution.py:64
  136.7 31.1 %copy-start.2 = (f32[1,8,128,128]{3,1,2,0:T(8,128)S(1)}, f32[1,8,128,128]{3,1,2,0:T(8,128)}, u32[]{:S(2)}) copy-start(f32[1,8,128,128]{3,1,2,0:T(8,128)} %get-tuple-element.16) | copy-start | bytes 1572868
  141.2 22.7 %all-to-all-start.3 = ((bf16[128,8,128]{2,1,0:T(8,128)(2,1)}), bf16[128,8,128]{2,1,0:T(8,128)(2,1)S(1)}, u32[]{:S(2)}, u32[]{:S(2)}) async-start(bf16[128,8,128]{2,1,0:T(8,128)(2,1)} %bitcast.19), calls=%async_computation.3 | async-start | bytes 524288 | tf_op jit(solution)/shard_map/all_to_all | solution.py:80
  164.0 23.8 %all-to-all-start = ((bf16[512,8,128]{2,1,0:T(8,128)(2,1)}), bf16[512,8,128]{2,1,0:T(8,128)(2,1)S(1)}, u32[]{:S(2)}, u32[]{:S(2)}) async-start(bf16[512,8,128]{2,1,0:T(8,128)(2,1)} %convert_element_type.72), calls=%async_computation | async-start | bytes 2097152 | tf_op jit(solution)/shard_map/all_to_all | solution.py:57
  175.4 13.1 %copy-start = (f32[8,16384]{1,0:T(8,128)S(1)}, f32[8,16384]{1,0:T(8,128)}, u32[]{:S(2)}) copy-start(f32[8,16384]{1,0:T(8,128)} %param.20) | copy-start | bytes 1572868
  323.1 19.4 %all-to-all-start.5 = ((f32[128,8,128]{2,1,0:T(8,128)}), f32[128,8,128]{2,1,0:T(8,128)S(1)}, u32[]{:S(2)}, u32[]{:S(2)}) async-start(f32[128,8,128]{2,1,0:T(8,128)} %fusion.5), calls=%async_computation.5 | async-start | bytes 1048576 | tf_op jit(solution)/shard_map/all_to_all | solution.py:76
  356.4 32.4 %all-to-all-start.6 = ((bf16[128,8,128]{2,1,0:T(8,128)(2,1)}), bf16[128,8,128]{2,1,0:T(8,128)(2,1)S(1)}, u32[]{:S(2)}, u32[]{:S(2)}) async-start(bf16[128,8,128]{2,1,0:T(8,128)(2,1)} %bitcast.30), calls=%async_computation.6 | async-start | bytes 524288 | tf_op jit(solution)/shard_map/all_to_all | solution.py:80
  388.8 29.5 %all-to-all-start.4 = ((bf16[512,8,128]{2,1,0:T(8,128)(2,1)}), bf16[512,8,128]{2,1,0:T(8,128)(2,1)S(1)}, u32[]{:S(2)}, u32[]{:S(2)}) async-start(bf16[512,8,128]{2,1,0:T(8,128)(2,1)} %convert_element_type.83), calls=%async_computation.4 | async-start | bytes 2097152 | tf_op jit(solution)/shard_map/all_to_all | solution.py:57
  409.6 10.8 %copy-start.1 = (f32[8,16384]{1,0:T(8,128)S(1)}, f32[8,16384]{1,0:T(8,128)}, u32[]{:S(2)}) copy-start(f32[8,16384]{1,0:T(8,128)} %get-tuple-element.12) | copy-start | bytes 1572868
where the time goes:
time: 550 us; the launch traced here: 548 us
  blocking collectives  339 us (62%)
  starting transfers between devices  53.1 us (10%)
  local copies, waits for them, and re-layouts  49.5 us (9%)
  matrix products  48.5 us (9%)
  waiting for transfers between devices  41.9 us (8%)
  other arithmetic  14.9 us (3%)
    psum x1, blocking collectives, local(): lax.psum(jnp.sum(right_side * right_side, axis=1), ('leaf', 'level'))  68.6 us
    psum x1, blocking collectives, local(): rest_sq = lax.psum(jnp.sum(remain * remain, axis=1), ('leaf', 'level'))  62.7 us
    psum x1, blocking collectives, local(): tail_sq = lax.psum(jnp.sum(leftover * leftover, axis=1), ('leaf', 'level'))  62.7 us
    psum x1, blocking collectives, local(): lax.psum(jnp.sum(basis_one * image_one, axis=1), ('leaf', 'level'))  62.7 us
    psum x1, blocking collectives, local(): lax.psum((jnp.sum(basis_one * image_two, axis=1), jnp.sum(basis_two * ima...  62.6 us
    scatter x2, local copies, waits for them, and re-layouts, near_field(): outgoing = jnp.zeros((groups * capacity, systems, points), jnp.float32).a...  23.8 us
    all_gather x2, blocking collectives, operator(): parent_table = lax.all_gather(parent_rows, 'level', axis=0, tiled=True)  20 us
    all_to_all x2, starting transfers between devices, downward(): lax.all_to_all(spread, ('leaf', 'level'), split_axis=0, concat_axis=0, ti...  19 us
  transfers between devices with their start and end apart: 7, of which 4 were waited for; matrix products, arithmetic and copies ran while one was open for 13% of the time, Pallas kernels for 0%

commit v1 on v0

--- a/solution.py
+++ b/solution.py
@@ -7,6 +7,7 @@
 
 
 EPSILON = 1e-06
+SCALE = 2.0**-20
 
 
 def local(
@@ -111,34 +112,80 @@
             "srk,spk->rsp", expanded, basis_slot, preferred_element_type=jnp.float32
         )
         far_sum = jnp.take(far_slot, inverse, axis=1)
-        total = 0.5 * vector_in.reshape(systems, clusters, points) + near_sum + far_sum
-        return total.reshape(systems, clusters * points)
-
-    sq_start = lax.psum(jnp.sum(right_side * right_side, axis=1), ("leaf", "level"))
-    start_norm = jnp.sqrt(sq_start + EPSILON)
-    basis_one = right_side / start_norm[:, None]
-    image_one = operator(basis_one)
-    along_one = lax.psum(jnp.sum(basis_one * image_one, axis=1), ("leaf", "level"))
-    remain = image_one - along_one[:, None] * basis_one
-    rest_sq = lax.psum(jnp.sum(remain * remain, axis=1), ("leaf", "level"))
-    rest_one = jnp.sqrt(rest_sq + EPSILON)
-    basis_two = remain / rest_one[:, None]
-    image_two = operator(basis_two)
-    cross_two, along_two = lax.psum(
-        (jnp.sum(basis_one * image_two, axis=1), jnp.sum(basis_two * image_two, axis=1)),
-        ("leaf", "level"),
-    )
-    leftover = image_two - cross_two[:, None] * basis_one - along_two[:, None] * basis_two
-    tail_sq = lax.psum(jnp.sum(leftover * leftover, axis=1), ("leaf", "level"))
+        return near_sum + far_sum
+
+    tiles = right_side.reshape(systems, clusters, points)
+    image = operator(tiles)
+    scaled = image * SCALE
+    second = operator(scaled)
+    own = jnp.stack(
+        [
+            jnp.sum(left * right, axis=(1, 2))
+            for left, right in (
+                (tiles, tiles),
+                (tiles, image),
+                (image, image),
+                (tiles, second),
+                (scaled, second),
+                (second, second),
+            )
+        ]
+    )
+    dots = jnp.sum(lax.all_gather(own, ("leaf", "level")), axis=0)
+    first_x, first_z, second_x, second_z, second_u = combine(dots)
+    solved = first_x[:, None, None] * tiles + first_z[:, None, None] * image
+    left_over = (
+        second_x[:, None, None] * tiles
+        + second_z[:, None, None] * image
+        + second_u[:, None, None] * second
+    )
+    return solved.reshape(systems, -1), left_over.reshape(systems, -1)
+
+
+def combine(dots):
+    start_sq = dots[0] + EPSILON
+    start_norm = jnp.sqrt(start_sq)
+    xx, xz, zz, xu, zu, uu = (dots[k] / start_sq for k in range(6))
+    along_one = 0.5 * xx + xz
+    kappa = along_one - 0.5
+    rest_raw = zz - 2.0 * kappa * xz + kappa * kappa * xx
+    rest_sq = rest_raw + EPSILON
+    rest_one = jnp.sqrt(rest_sq)
+    scaled_rest = SCALE * rest_one
+    scaled_sq = scaled_rest * scaled_rest
+    xzs = SCALE * xz
+    zzs = SCALE * SCALE * zz
+    beta = (xz - kappa * xx) / rest_one
+    gamma = rest_raw / rest_sq
+    one_t = (xu - kappa * xzs) / scaled_rest
+    two_t = (zu - kappa * zzs - SCALE * kappa * (xu - kappa * xzs)) / scaled_sq
+    t_t = (uu - 2.0 * kappa * zu + kappa * kappa * zzs) / scaled_sq
+    cross_two = 0.5 * beta + one_t
+    along_two = 0.5 * gamma + two_t
+    short = 0.5 - along_two
+    tail_sq = (
+        t_t
+        + short * short * gamma
+        + cross_two * cross_two * xx
+        + 2.0 * short * two_t
+        - 2.0 * cross_two * one_t
+        - 2.0 * cross_two * short * beta
+    )
     gram_first = along_one * along_one + rest_one * rest_one
     gram_cross = along_one * cross_two + rest_one * along_two
     gram_last = cross_two * cross_two + along_two * along_two + tail_sq
     determinant = gram_first * gram_last - gram_cross * gram_cross
     coef_one = start_norm * (along_one * gram_last - cross_two * gram_cross) / determinant
     coef_two = start_norm * (gram_first * cross_two - gram_cross * along_one) / determinant
-    solution = coef_one[:, None] * basis_one + coef_two[:, None] * basis_two
-    residual = right_side - coef_one[:, None] * image_one - coef_two[:, None] * image_two
-    return (solution, residual)
+    one = coef_one / start_norm
+    two = coef_two / (start_norm * rest_one)
+    return (
+        one - kappa * two,
+        two,
+        1.0 - 0.5 * one + 0.5 * kappa * two,
+        -one - (0.5 - kappa) * two,
+        -coef_two / (start_norm * scaled_rest),
+    )
 
 
 def solution(mesh):

time: 550 us -> 273 us (0.50)
  blocking collectives: 339 us -> 73 us
  local copies, waits for them, and re-layouts: 49.5 us -> 38.8 us
  other arithmetic: 14.9 us -> 7.56 us
    psum x5 -> x0, blocking collectives: 319 us -> none  [the longest x1 68.6 us: local(): lax.psum(jnp.sum(right_side * right_side, axis=1), ('leaf', 'level'))]
    all_gather x0 -> x1, blocking collectives: none -> 53 us  [local(): dots = jnp.sum(lax.all_gather(own, ('leaf', 'level')), axis=0)]
    scatter x2, local copies, waits for them, and re-layouts: 23.8 us -> 14.1 us  [near_field(): outgoing = jnp.zeros((groups * capacity, systems, points), jnp.float32).a...]
  transfers between devices with their start and end apart: 7 -> 7, of which waited for: 4 -> 4; matrix products, arithmetic and copies ran while one was open for 13% -> 19% of each run, Pallas kernels for 0% -> 0%
where the time goes in v1:
time: 273 us; the launch traced here: 272 us
  blocking collectives  73 us (27%)
  starting transfers between devices  58.5 us (21%)
  waiting for transfers between devices  47.3 us (17%)
  matrix products  45.6 us (17%)
  local copies, waits for them, and re-layouts  38.8 us (14%)
  other arithmetic  7.56 us (3%)
    all_gather x1, blocking collectives, local(): dots = jnp.sum(lax.all_gather(own, ('leaf', 'level')), axis=0)  53 us
    all_to_all x2, waiting for transfers between devices, near_field(): lax.all_to_all(outgoing.astype(jnp.bfloat16), ('leaf', 'level'), split_ax...  22.5 us
    all_gather x2, blocking collectives, operator(): parent_table = lax.all_gather(parent_rows, 'level', axis=0, tiled=True)  20 us
    all_to_all x2, starting transfers between devices, downward(): lax.all_to_all(spread, ('leaf', 'level'), split_axis=0, concat_axis=0, ti...  19 us
    all_to_all x2, starting transfers between devices, upward(): lax.all_to_all(lifted, ('leaf', 'level'), split_axis=0, concat_axis=0, ti...  15.6 us
    all_to_all x2, starting transfers between devices, near_field(): lax.all_to_all(outgoing.astype(jnp.bfloat16), ('leaf', 'level'), split_ax...  14.1 us
    scatter x2, local copies, waits for them, and re-layouts, near_field(): outgoing = jnp.zeros((groups * capacity, systems, points), jnp.float32).a...  14.1 us
    dot_general x2, matrix products, operator(): jnp.einsum('srk,spk->rsp', expanded, basis_slot, preferred_element_type=j...  13.9 us
  transfers between devices with their start and end apart: 7, of which 4 were waited for; matrix products, arithmetic and copies ran while one was open for 19% of the time, Pallas kernels for 0%

profile of v1, /device:TPU:1, one launch (start us, length us, event | category | flops | bytes accessed | tf_op | source)
XLA Modules:
  0.0 271.7 jit_solution(17496570078938637699)
XLA Ops:
  3.9 5.2 %gather_fusion.3 = bf16[128,128,128]{2,1,0:T(8,128)(2,1)} fusion(bf16[128,128,128]{2,1,0:T(8,128)(2,1)} %param.22, s32[1024]{0:T(1024)S(1)} %pad_clamp_fusion.2), kind=kCustom, calls=%fused_computation.6.clone | custom fusion | bytes 8389120 | tf_op jit(solution)/shard_map/jit(_take)/gather | solution.py:35
  9.2 5.2 %gather_fusion.1 = bf16[128,128,128]{2,1,0:T(8,128)(2,1)} fusion(bf16[128,128,128]{2,1,0:T(8,128)(2,1)} %param.21, s32[1024]{0:T(1024)S(1)} %pad_clamp_fusion.2), kind=kCustom, calls=%fused_computation.1.clone | custom fusion | bytes 8389120 | tf_op jit(solution)/shard_map/jit(_take)/gather | solution.py:34
  14.4 6.7 %fusion.2 = f32[128,8,128]{2,1,0:T(8,128)} fusion(bf16[128,8,128]{2,1,0:T(8,128)(2,1)S(1)} %gather_fusion.2, pred[128]{0:T(512)(128)(4,1)S(1)} %compare_and_fusion.2, bf16[128,128,128]{2,1,0:T(8,128)(2,1)} %gather_fusion.1, bf16[128,128,128]{2,1,0:T(8,128)(2,1)} %gather_fusion.3), kind=kOutput, calls=%fused_computation.26 | convolution fusion | flops 71565312 | bytes 9175168 | tf_op jit(solution)/shard_map/srk,skj->srj/dot_general | solution.py:93
  21.1 12.0 %all-to-all-start.2 = ((f32[128,8,128]{2,1,0:T(8,128)}), f32[128,8,128]{2,1,0:T(8,128)}, u32[]{:S(2)}, u32[]{:S(2)}) async-start(f32[128,8,128]{2,1,0:T(8,128)} %fusion.2), calls=%async_computation.2 | async-start | bytes 1048576 | tf_op jit(solution)/shard_map/all_to_all | solution.py:77
  36.9 4.7 %fusion.10 = f32[256,8,128]{2,1,0:T(8,128)S(1)} fusion(bf16[256,128,128]{2,1,0:T(8,128)(2,1)} %param.29, bf16[256,8,128]{2,1,0:T(8,128)(2,1)S(1)} %gather_fusion, pred[256]{0:T(512)(128)(4,1)S(1)} %compare_and_fusion.3), kind=kOutput, calls=%fused_computation.41 | convolution fusion | flops 67371008 | bytes 9961728 | tf_op jit(solution)/shard_map/rnp,npq->nrq/dot_general | solution.py:49
  41.8 7.0 %scatter_fusion = f32[512,8,128]{2,1,0:T(8,128)S(1)} fusion(f32[512,8,128]{2,1,0:T(8,128)S(1)} %broadcast.333.clone, s32[256]{0:T(256)S(1)} %bitcast.177, f32[256,8,128]{2,1,0:T(8,128)S(1)} %fusion.10), kind=kCustom, calls=%fused_computation.10 | custom fusion | bytes 3146752 | tf_op jit(solution)/shard_map/scatter | solution.py:55
  51.1 9.8 %all-to-all-start.1 = ((bf16[128,4,1]{1,2,0:T(2,128)(2,1)}), bf16[128,4,1]{1,2,0:T(2,128)(2,1)S(1)}, u32[]{:S(2)}, u32[]{:S(2)}) async-start(bf16[128,4,1]{1,2,0:T(2,128)(2,1)} %all_to_all.33), calls=%async_computation.1 | async-start | bytes 131072 | tf_op jit(solution)/shard_map/all_to_all | solution.py:65
  61.9 10.6 %all_gather.12 = bf16[128,8,128]{2,1,0:T(8,128)(2,1)S(1)} all-gather(bf16[32,8,128]{2,1,0:T(8,128)(2,1)S(1)} %bitcast_reduce_fusion.1), channel_id=1, replica_groups=mesh['leaf'=32,'level'=4] {'level'}, dimensions={0}, use_global_device_ids=true | all-gather | bytes 327680 | tf_op jit(solution)/shard_map/all_gather | solution.py:100
  77.0 11.4 %all-to-all-start.3 = ((bf16[128,8,128]{2,1,0:T(8,128)(2,1)}), bf16[128,8,128]{2,1,0:T(8,128)(2,1)S(1)}, u32[]{:S(2)}, u32[]{:S(2)}) async-start(bf16[128,8,128]{2,1,0:T(8,128)(2,1)} %bitcast.20), calls=%async_computation.3 | async-start | bytes 524288 | tf_op jit(solution)/shard_map/all_to_all | solution.py:81
  88.5 11.3 %all-to-all-done.3 = bf16[128,8,128]{2,1,0:T(8,128)(2,1)S(1)} async-done(((bf16[128,8,128]{2,1,0:T(8,128)(2,1)}), bf16[128,8,128]{2,1,0:T(8,128)(2,1)S(1)}, u32[]{:S(2)}, u32[]{:S(2)}) %all-to-all-start.3) | async-done | bytes 262176 | tf_op jit(solution)/shard_map/all_to_all | solution.py:81
  99.8 3.9 %all-to-all-start = ((bf16[512,8,128]{2,1,0:T(8,128)(2,1)}), bf16[512,8,128]{2,1,0:T(8,128)(2,1)S(1)}, u32[]{:S(2)}, u32[]{:S(2)}) async-start(bf16[512,8,128]{2,1,0:T(8,128)(2,1)} %convert_element_type.72), calls=%async_computation | async-start | bytes 2097152 | tf_op jit(solution)/shard_map/all_to_all | solution.py:58
  104.0 6.9 %convolution_bitcast_fusion.1 = f32[8,128,128]{2,0,1:T(8,128)S(1)} fusion(bf16[128,8,128]{2,1,0:T(8,128)(2,1)S(1)} %all-to-all-done.3, bf16[128,128,128]{2,1,0:T(8,128)(2,1)} %gather_fusion.1, pred[128]{0:T(512)(128)(4,1)S(1)} %compare_and_fusion.2, bf16[128,128,128]{2,1,0:T(8,128)(2,1)} %gather_fusion.3), kind=kOutput, calls=%fused_computation.17 | convolution fusion | flops 71434240 | bytes 9175168 | tf_op jit(solution)/shard_map/srk,spk->rsp/dot_general | solution.py:111
  111.9 11.5 %all-to-all-done = bf16[512,8,128]{2,1,0:T(8,128)(2,1)S(1)} async-done(((bf16[512,8,128]{2,1,0:T(8,128)(2,1)}), bf16[512,8,128]{2,1,0:T(8,128)(2,1)S(1)}, u32[]{:S(2)}, u32[]{:S(2)}) %all-to-all-start) | async-done | bytes 1048608 | tf_op jit(solution)/shard_map/all_to_all | solution.py:58
  125.6 6.6 %fusion.3 = f32[128,8,128]{2,1,0:T(8,128)} fusion(bf16[128,8,128]{2,1,0:T(8,128)(2,1)S(1)} %gather_fusion.7, pred[128]{0:T(512)(128)(4,1)S(1)} %compare_and_fusion.2, bf16[128,128,128]{2,1,0:T(8,128)(2,1)} %gather_fusion.1, bf16[128,128,128]{2,1,0:T(8,128)(2,1)} %gather_fusion.3), kind=kOutput, calls=%fused_computation.27 | convolution fusion | flops 71565312 | bytes 9175168 | tf_op jit(solution)/shard_map/srk,skj->srj/dot_general | solution.py:93
  132.3 3.7 %all-to-all-start.5 = ((f32[128,8,128]{2,1,0:T(8,128)}), f32[128,8,128]{2,1,0:T(8,128)S(1)}, u32[]{:S(2)}, u32[]{:S(2)}) async-start(f32[128,8,128]{2,1,0:T(8,128)} %fusion.3), calls=%async_computation.5 | async-start | bytes 1048576 | tf_op jit(solution)/shard_map/all_to_all | solution.py:77
  136.7 13.5 %all-to-all-done.5 = f32[128,8,128]{2,1,0:T(8,128)S(1)} async-done(((f32[128,8,128]{2,1,0:T(8,128)}), f32[128,8,128]{2,1,0:T(8,128)S(1)}, u32[]{:S(2)}, u32[]{:S(2)}) %all-to-all-start.5) | async-done | bytes 524320 | tf_op jit(solution)/shard_map/all_to_all | solution.py:77
  150.2 9.4 %all_gather.13 = bf16[128,8,128]{2,1,0:T(8,128)(2,1)S(1)} all-gather(bf16[32,8,128]{2,1,0:T(8,128)(2,1)S(1)} %bitcast_reduce_fusion), channel_id=1, replica_groups=mesh['leaf'=32,'level'=4] {'level'}, dimensions={0}, use_global_device_ids=true | all-gather | bytes 327680 | tf_op jit(solution)/shard_map/all_gather | solution.py:100
  164.1 7.6 %all-to-all-start.6 = ((bf16[128,8,128]{2,1,0:T(8,128)(2,1)}), bf16[128,8,128]{2,1,0:T(8,128)(2,1)S(1)}, u32[]{:S(2)}, u32[]{:S(2)}) async-start(bf16[128,8,128]{2,1,0:T(8,128)(2,1)} %bitcast.32), calls=%async_computation.6 | async-start | bytes 524288 | tf_op jit(solution)/shard_map/all_to_all | solution.py:81
  171.7 4.7 %fusion.8 = f32[256,8,128]{2,1,0:T(8,128)S(1)} fusion(bf16[256,128,128]{2,1,0:T(8,128)(2,1)} %param.29, bf16[256,8,128]{2,1,0:T(8,128)(2,1)S(1)} %gather_fusion.6, pred[256]{0:T(512)(128)(4,1)S(1)} %compare_and_fusion.3), kind=kOutput, calls=%fused_computation.38 | convolution fusion | flops 67371008 | bytes 9961728 | tf_op jit(solution)/shard_map/rnp,npq->nrq/dot_general | solution.py:49
  176.6 7.0 %scatter_fusion.1 = f32[512,8,128]{2,1,0:T(8,128)S(1)} fusion(f32[512,8,128]{2,1,0:T(8,128)S(1)} %broadcast.333, s32[256]{0:T(256)S(1)} %bitcast.178, f32[256,8,128]{2,1,0:T(8,128)S(1)} %fusion.8), kind=kCustom, calls=%fused_computation.13 | custom fusion | bytes 3146752 | tf_op jit(solution)/shard_map/scatter | solution.py:55
  184.7 10.2 %all-to-all-start.4 = ((bf16[512,8,128]{2,1,0:T(8,128)(2,1)}), bf16[512,8,128]{2,1,0:T(8,128)(2,1)}, u32[]{:S(2)}, u32[]{:S(2)}) async-start(bf16[512,8,128]{2,1,0:T(8,128)(2,1)} %convert_element_type.83), calls=%async_computation.4 | async-start | bytes 2097152 | tf_op jit(solution)/shard_map/all_to_all | solution.py:58
  195.3 7.0 %convolution_bitcast_fusion = f32[8,128,128]{2,0,1:T(8,128)S(1)} fusion(bf16[128,8,128]{2,1,0:T(8,128)(2,1)S(1)} %all-to-all-done.6, bf16[128,128,128]{2,1,0:T(8,128)(2,1)} %gather_fusion.1, pred[128]{0:T(512)(128)(4,1)S(1)} %compare_and_fusion.2, bf16[128,128,128]{2,1,0:T(8,128)(2,1)} %gather_fusion.3), kind=kOutput, calls=%fused_computation.16 | convolution fusion | flops 71434240 | bytes 9175168 | tf_op jit(solution)/shard_map/srk,spk->rsp/dot_general | solution.py:111
  203.3 11.0 %all-to-all-done.4 = bf16[512,8,128]{2,1,0:T(8,128)(2,1)} async-done(((bf16[512,8,128]{2,1,0:T(8,128)(2,1)}), bf16[512,8,128]{2,1,0:T(8,128)(2,1)}, u32[]{:S(2)}, u32[]{:S(2)}) %all-to-all-start.4) | async-done | bytes 1048608 | tf_op jit(solution)/shard_map/all_to_all | solution.py:58
  216.3 53.0 %all-gather.1 = f32[128,6,8]{2,1,0:T(8,128)S(1)} all-gather(f32[1,6,8]{2,1,0:T(8,128)S(1)} %bitcast.172), channel_id=2, replica_groups=mesh['leaf'=32,'level'=4] {'leaf','level'}, dimensions={0}, use_global_device_ids=true | all-gather | bytes 24768 | tf_op jit(solution)/shard_map/all_gather | solution.py:134
  (89 shorter events, 30.8 us)
Async XLA Ops:
  14.4 18.6 %copy-start.6 = (s32[1,128]{1,0:T(1,128)S(1)}, s32[1,128]{1,0:T(1,128)}, u32[]{:S(2)}) copy-start(s32[1,128]{1,0:T(1,128)} %param.23) | copy-start | bytes 1540
  14.4 18.7 %copy-start.4 = (s32[256]{0:T(256)S(1)}, s32[256]{0:T(256)}, u32[]{:S(2)}) copy-start(s32[256]{0:T(256)} %param.26) | copy-start | bytes 3076
  14.4 18.7 %copy-start.5 = (s32[256]{0:T(256)S(1)}, s32[256]{0:T(256)}, u32[]{:S(2)}) copy-start(s32[256]{0:T(256)} %param.28) | copy-start | bytes 3076
  14.4 18.7 %copy-start.3 = (s32[32,4]{0,1:T(4,128)S(1)}, s32[32,4]{0,1:T(4,128)}, u32[]{:S(2)}) copy-start(s32[32,4]{0,1:T(4,128)} %param.24) | copy-start | bytes 1540
  14.4 18.9 %copy-start.2 = (s32[256,1]{0,1:T(1,128)S(1)}, s32[256,1]{0,1:T(1,128)}, u32[]{:S(2)}) copy-start(s32[256,1]{0,1:T(1,128)} %param.27) | copy-start | bytes 3076
  21.1 30.0 %all-to-all-start.2 = ((f32[128,8,128]{2,1,0:T(8,128)}), f32[128,8,128]{2,1,0:T(8,128)}, u32[]{:S(2)}, u32[]{:S(2)}) async-start(f32[128,8,128]{2,1,0:T(8,128)} %fusion.2), calls=%async_computation.2 | async-start | bytes 1048576 | tf_op jit(solution)/shard_map/all_to_all | solution.py:77
  51.1 25.2 %all-to-all-start.1 = ((bf16[128,4,1]{1,2,0:T(2,128)(2,1)}), bf16[128,4,1]{1,2,0:T(2,128)(2,1)S(1)}, u32[]{:S(2)}, u32[]{:S(2)}) async-start(bf16[128,4,1]{1,2,0:T(2,128)(2,1)} %all_to_all.33), calls=%async_computation.1 | async-start | bytes 131072 | tf_op jit(solution)/shard_map/all_to_all | solution.py:65
  77.0 22.7 %all-to-all-start.3 = ((bf16[128,8,128]{2,1,0:T(8,128)(2,1)}), bf16[128,8,128]{2,1,0:T(8,128)(2,1)S(1)}, u32[]{:S(2)}, u32[]{:S(2)}) async-start(bf16[128,8,128]{2,1,0:T(8,128)(2,1)} %bitcast.20), calls=%async_computation.3 | async-start | bytes 524288 | tf_op jit(solution)/shard_map/all_to_all | solution.py:81
  99.8 23.6 %all-to-all-start = ((bf16[512,8,128]{2,1,0:T(8,128)(2,1)}), bf16[512,8,128]{2,1,0:T(8,128)(2,1)S(1)}, u32[]{:S(2)}, u32[]{:S(2)}) async-start(bf16[512,8,128]{2,1,0:T(8,128)(2,1)} %convert_element_type.72), calls=%async_computation | async-start | bytes 2097152 | tf_op jit(solution)/shard_map/all_to_all | solution.py:58
  132.3 17.9 %all-to-all-start.5 = ((f32[128,8,128]{2,1,0:T(8,128)}), f32[128,8,128]{2,1,0:T(8,128)S(1)}, u32[]{:S(2)}, u32[]{:S(2)}) async-start(f32[128,8,128]{2,1,0:T(8,128)} %fusion.3), calls=%async_computation.5 | async-start | bytes 1048576 | tf_op jit(solution)/shard_map/all_to_all | solution.py:77
  164.1 20.6 %all-to-all-start.6 = ((bf16[128,8,128]{2,1,0:T(8,128)(2,1)}), bf16[128,8,128]{2,1,0:T(8,128)(2,1)S(1)}, u32[]{:S(2)}, u32[]{:S(2)}) async-start(bf16[128,8,128]{2,1,0:T(8,128)(2,1)} %bitcast.32), calls=%async_computation.6 | async-start | bytes 524288 | tf_op jit(solution)/shard_map/all_to_all | solution.py:81
  183.6 11.3 %copy-start.1 = (f32[8,16384]{1,0:T(8,128)S(1)}, f32[8,16384]{1,0:T(8,128)}, u32[]{:S(2)}) copy-start(f32[8,16384]{1,0:T(8,128)} %param.20) | copy-start | bytes 1572868
  184.7 29.6 %all-to-all-start.4 = ((bf16[512,8,128]{2,1,0:T(8,128)(2,1)}), bf16[512,8,128]{2,1,0:T(8,128)(2,1)}, u32[]{:S(2)}, u32[]{:S(2)}) async-start(bf16[512,8,128]{2,1,0:T(8,128)(2,1)} %convert_element_type.83), calls=%async_computation.4 | async-start | bytes 2097152 | tf_op jit(solution)/shard_map/all_to_all | solution.py:58
  195.3 19.1 %copy-start = (f32[8,128,128]{1,2,0:T(8,128)S(1)}, f32[8,128,128]{1,2,0:T(8,128)}, u32[]{:S(2)}) copy-start(f32[8,128,128]{1,2,0:T(8,128)} %get-tuple-element.34) | copy-start | bytes 1572868

commit v2 on v1

v2 whole, which is shorter than its diff:
```python
import functools

import jax
import jax.numpy as jnp
from jax import lax
from jax.experimental import pallas as pl
from jax.experimental.pallas import tpu as pltpu
from jax.sharding import PartitionSpec as P

CHILDREN = 4
CAPACITY = 4
EPSILON = 1e-06
SCALE = 2.0**-20
AXES = ("leaf", "level")
LOGICAL = pl.DeviceIdType.LOGICAL
F32 = jnp.float32
BF16 = jnp.bfloat16


def combine(dots):
    start_sq = dots[0] + EPSILON
    start_norm = jnp.sqrt(start_sq)
    xx, xzs, zzs, xu, zu, uu = (dots[k] / start_sq for k in range(6))
    xz = xzs / SCALE
    zz = zzs / (SCALE * SCALE)
    along_one = 0.5 * xx + xz
    kappa = along_one - 0.5
    rest_raw = zz - 2.0 * kappa * xz + kappa * kappa * xx
    rest_sq = rest_raw + EPSILON
    rest_one = jnp.sqrt(rest_sq)
    scaled_rest = SCALE * rest_one
    scaled_sq = scaled_rest * scaled_rest
    beta = (xz - kappa * xx) / rest_one
    gamma = rest_raw / rest_sq
    one_t = (xu - kappa * xzs) / scaled_rest
    two_t = (zu - kappa * zzs - SCALE * kappa * (xu - kappa * xzs)) / scaled_sq
    t_t = (uu - 2.0 * kappa * zu + kappa * kappa * zzs) / scaled_sq
    cross_two = 0.5 * beta + one_t
    along_two = 0.5 * gamma + two_t
    short = 0.5 - along_two
    tail_sq = (
        t_t
        + short * short * gamma
        + cross_two * cross_two * xx
        + 2.0 * short * two_t
        - 2.0 * cross_two * one_t
        - 2.0 * cross_two * short * beta
    )
    gram_first = along_one * along_one + rest_one * rest_one
    gram_cross = along_one * cross_two + rest_one * along_two
    gram_last = cross_two * cross_two + along_two * along_two + tail_sq
    determinant = gram_first * gram_last - gram_cross * gram_cross
    coef_one = start_norm * (along_one * gram_last - cross_two * gram_cross) / determinant
    coef_two = start_norm * (gram_first * cross_two - gram_cross * along_one) / determinant
    one = coef_one / start_norm
    two = coef_two / (start_norm * rest_one)
    scaled_two = coef_two / (start_norm * scaled_rest)
    return (
        one - kappa * two,
        scaled_two,
        1.0 - 0.5 * one + 0.5 * kappa * two,
        -one / SCALE - (0.5 - kappa) * scaled_two,
        -scaled_two,
    )


def loop(count, unroll, body):
    def step(block, carry):
        for u in range(unroll):
            body(block * unroll + u)
        return carry

    lax.fori_loop(0, count // unroll, step, 0)


def kernel(
    target_ref, order_ref, far_ref, inverse_ref, source_ref, perm_ref, keep_ref, last_ref,
    x_hbm, basis_hbm, transfer_hbm, far_hbm, near_hbm,
    solved_ref, left_ref,
    x_ref, z_ref, u_ref, basis_ref, transfer_ref, product_ref, far_w, near_w,
    part_ref, lifted_ref, field_ref, run_ref,
    up_send, up_recv, down_send, near_send,
    table_one, table_two, down_one, down_two, near_one, near_two, cast_one, cast_two,
    dot_send, dot_recv,
    load_sem, remote_sem,
):
    clusters = basis_ref.shape[0]
    devices = clusters
    levels = lax.axis_size("level")
    leaf, level = lax.axis_index("leaf"), lax.axis_index("level")
    me = leaf * levels + level
    pairs = near_w.shape[0]
    parents = clusters // CHILDREN
    partners = far_w.shape[0] // parents
    lanes = basis_ref.shape[1]
    chunks = 8
    rows = clusters // chunks

    loads = [pltpu.make_async_copy(x_hbm, x_ref, load_sem.at[0])]
    for k in range(chunks):
        part = pl.ds(k * rows, rows)
        loads.append(
            pltpu.make_async_copy(basis_hbm.at[part], basis_ref.at[part], load_sem.at[1 + 2 * k])
        )
        loads.append(
            pltpu.make_async_copy(
                transfer_hbm.at[part], transfer_ref.at[part], load_sem.at[2 + 2 * k]
            )
        )
    load_near = pltpu.make_async_copy(near_hbm, near_w, load_sem.at[1 + 2 * chunks])
    load_far = pltpu.make_async_copy(far_hbm, far_w, load_sem.at[2 + 2 * chunks])
    for copy in loads:
        copy.start()
    load_near.start()
    load_far.start()

    barrier = pltpu.get_barrier_semaphore()

    def greet(i, carry):
        pl.semaphore_signal(
            barrier, inc=1, device_id=(me + i) % devices, device_id_type=LOGICAL
        )
        return carry

    lax.fori_loop(1, devices, greet, 0, unroll=8)

    def push(src, dst, stage, device):
        pltpu.make_async_remote_copy(
            src_ref=src,
            dst_ref=dst,
            send_sem=remote_sem.at[stage, 0],
            recv_sem=remote_sem.at[stage, 1],
            device_id=device,
            device_id_type=LOGICAL,
        ).start()

    def settle(ref, stage):
        for end in range(2):
            pltpu.make_async_copy(ref, ref, remote_sem.at[stage, end]).wait()

    def push_all(lo, hi, stage, src, dst):
        def go(i, carry):
            other = (me + i) % devices
            push(src(other), dst, stage, other)
            return carry

        lax.fori_loop(lo, hi, go, 0, unroll=8)

    def tile(ref, c):
        return ref[:, pl.ds(pl.multiple_of(c * lanes, lanes), lanes)]

    run_ref[CAPACITY * devices] = jnp.zeros(run_ref.shape[1:], F32)

    for trip, (v_ref, o_ref, scale) in enumerate(((x_ref, z_ref, SCALE), (z_ref, u_ref, 1.0))):
        first = trip == 0
        stage = 4 * trip
        table_ref = table_one if first else table_two
        down_recv = down_one if first else down_two
        near_recv = near_one if first else near_two
        cast_ref = cast_one if first else cast_two

        def lift(c):
            value = tile(v_ref, c).astype(BF16)
            cast_ref[c] = value
            lifted_ref[c] = jnp.dot(value, product_ref[c], preferred_element_type=F32)

        if first:
            loads[0].wait()

            for k in range(chunks):
                loads[1 + 2 * k].wait()
                loads[2 + 2 * k].wait()

                def fuse(c, k=k):
                    product_ref[k * rows + c] = jnp.dot(
                        basis_ref[k * rows + c],
                        transfer_ref[k * rows + c],
                        preferred_element_type=F32,
                    ).astype(BF16)

                loop(rows, 8, fuse)
        loop(clusters, 16, lift)

        def order_up(s):
            up_send[trip, s] = lifted_ref[order_ref[s]].astype(BF16)

        loop(clusters, 16, order_up)
        up_recv[trip, me] = lifted_ref[order_ref[me]].astype(BF16)
        if first:
            pl.semaphore_wait(barrier, devices - 1)
        push_all(1, devices, stage, lambda e: up_send.at[trip, e], up_recv.at[trip, me])

        if first:
            load_near.wait()

        def near_product(n):
            part_ref[n] = jnp.dot(
                cast_ref[target_ref[n]], near_w[n], preferred_element_type=F32
            )

        loop(pairs, 32, near_product)

        def place(s):
            near_send[trip, s] = part_ref[source_ref[s]].astype(BF16)

        loop(CAPACITY * devices, 16, place)
        for k in range(CAPACITY):
            near_recv[CAPACITY * me + k] = part_ref[
                source_ref[CAPACITY * me + k]
            ].astype(BF16)

        def near_push(lo, hi):
            push_all(
                lo,
                hi,
                stage + 3,
                lambda e: near_send.at[trip, pl.ds(CAPACITY * e, CAPACITY)],
                near_recv.at[pl.ds(CAPACITY * me, CAPACITY)],
            )

        near_push(1, 43)
        settle(up_recv.at[trip, pl.ds(0, devices - 1)], stage)

        def gather_parent(q):
            total = up_recv[trip, CHILDREN * q].astype(F32)
            for i in range(1, CHILDREN):
                total = total + up_recv[trip, CHILDREN * q + i].astype(F32)
            table_ref[level * parents + q] = total.astype(BF16)

        loop(parents, 8, gather_parent)
        mine = table_ref.at[pl.ds(level * parents, parents)]
        for i in range(1, CHILDREN):
            push(mine, mine, stage + 1, leaf * levels + (level + i) % levels)
        near_push(43, 85)
        if first:
            load_far.wait()
        settle(table_ref.at[pl.ds(0, (levels - 1) * parents)], stage + 1)

        def translate(q):
            picked = jnp.concatenate(
                [table_ref[far_ref[partners * q + k]] for k in range(partners)], axis=1
            )
            mats = far_w[pl.ds(partners * q, partners)].reshape(partners * lanes, lanes)
            down_send[trip, q] = jnp.dot(picked, mats, preferred_element_type=F32).astype(BF16)

        loop(parents, 8, translate)
        down_recv[me] = down_send[trip, me // CHILDREN]
        push_all(
            1, devices, stage + 2, lambda e: down_send.at[trip, e // CHILDREN], down_recv.at[me]
        )
        near_push(85, devices)
        settle(down_recv.at[pl.ds(0, devices - 1)], stage + 2)

        def spread(c):
            field_ref[c] = lax.dot_general(
                down_recv[inverse_ref[c]],
                product_ref[c],
                (((1,), (1,)), ((), ())),
                preferred_element_type=F32,
            )

        loop(clusters, 16, spread)
        settle(near_recv.at[pl.ds(0, CAPACITY * (devices - 1))], stage + 3)

        def land(block, total):
            for u in range(8):
                i = block * 8 + u
                total = total * keep_ref[i].astype(F32) + near_recv[perm_ref[i]].astype(F32)
                run_ref[i] = total
            return total

        lax.fori_loop(0, CAPACITY * devices // 8, land, jnp.zeros(run_ref.shape[1:], F32))

        def finish(c):
            value = field_ref[c] + run_ref[last_ref[c]]
            if scale != 1.0:
                value = value * scale
            o_ref[:, pl.ds(pl.multiple_of(c * lanes, lanes), lanes)] = value

        loop(clusters, 16, finish)

    systems = x_ref.shape[0]

    def products(block, sums):
        sums = list(sums)
        for u in range(4):
            x, z, w = (tile(ref, block * 4 + u) for ref in (x_ref, z_ref, u_ref))
            for k, (a, b) in enumerate(((x, x), (x, z), (z, z), (x, w), (z, w), (w, w))):
                sums[k] = sums[k] + a * b
        return tuple(sums)

    zero = jnp.zeros((systems, lanes), F32)
    sums = lax.fori_loop(0, clusters // 4, products, (zero,) * 6)
    lane = lax.broadcasted_iota(jnp.int32, (systems, lanes), 1)
    row = lax.broadcasted_iota(jnp.int32, (systems, lanes), 0)
    packed = zero
    for k, total in enumerate(sums):
        packed = jnp.where(
            lane == row + k * systems, jnp.sum(total, axis=1, keepdims=True), packed
        )
    packed = jnp.sum(packed, axis=0, keepdims=True)
    dot_send[...] = packed
    dot_recv[pl.ds(me, 1)] = packed[None]
    push_all(1, devices, 8, lambda e: dot_send, dot_recv.at[me])
    for end, ref in ((0, dot_recv), (1, dot_recv)):
        ref = ref.at[pl.ds(0, devices - 1)]
        pltpu.make_async_copy(ref, ref, remote_sem.at[8, end]).wait()
    gathered = jnp.sum(dot_recv[...], axis=0)
    spread_out = jnp.broadcast_to(gathered, (systems, lanes))
    dots = [
        jnp.sum(jnp.where(lane == row + k * systems, spread_out, 0.0), axis=1, keepdims=True)
        for k in range(6)
    ]
    first_x, first_z, second_x, second_z, second_u = (
        jnp.broadcast_to(value, (systems, lanes)) for value in combine(dots)
    )

    def write(c):
        where = pl.ds(pl.multiple_of(c * lanes, lanes), lanes)
        x, z, w = x_ref[:, where], z_ref[:, where], u_ref[:, where]
        solved_ref[:, where] = first_x * x + first_z * z
        left_ref[:, where] = second_x * x + second_z * z + second_u * w

    loop(clusters, 8, write)


def local(
    right_side,
    basis,
    transfer,
    order,
    far_src,
    far_mats,
    near_target,
    near_dest,
    near_src,
    near_blocks,
):
    systems, panels = right_side.shape
    clusters, points, coeffs = basis.shape
    devices = lax.axis_size(AXES)
    pairs = near_target.shape[0]
    parents = clusters // CHILDREN
    slots = CAPACITY * devices

    def ints(values):
        return values.astype(jnp.int32)

    index = jnp.arange(clusters, dtype=jnp.int32)
    inverse = jnp.sum(ints(order[0][None, :] == index[:, None]) * index[None, :], axis=1)
    dest = near_dest[:, 0]
    number = jnp.arange(pairs, dtype=jnp.int32)
    rank = jnp.sum(ints((dest[None, :] == dest[:, None]) & (number[None, :] < number[:, None])), axis=1)
    slot = dest * CAPACITY + rank
    every = jnp.arange(slots, dtype=jnp.int32)
    here = ints(slot[None, :] == every[:, None])
    source = jnp.sum(here * number[None, :], axis=1)
    label = jnp.sum(here * (near_src[None, :] - clusters), axis=1) + clusters
    labels = lax.all_to_all(
        label.reshape(devices, CAPACITY), AXES, split_axis=0, concat_axis=0, tiled=True
    ).reshape(slots)
    less = ints(labels[None, :] < labels[:, None])
    tied = ints((labels[None, :] == labels[:, None]) & (every[None, :] < every[:, None]))
    below = jnp.sum(less, axis=1)
    position = below + jnp.sum(tied, axis=1)
    there = ints(position[None, :] == every[:, None])
    perm = jnp.sum(there * every[None, :], axis=1)
    keep = ints(jnp.sum(there * below[None, :], axis=1) != every)
    upto = jnp.sum(ints(labels[None, :] <= index[:, None]), axis=1)
    some = jnp.sum(ints(labels[None, :] == index[:, None]), axis=1)
    last = jnp.where(some > 0, upto - 1, slots)

    smem = pl.BlockSpec(memory_space=pltpu.SMEM)
    hbm = pl.BlockSpec(memory_space=pl.ANY)
    vmem = pl.BlockSpec(memory_space=pltpu.VMEM)
    field = jax.ShapeDtypeStruct((systems, panels), F32)
    cell = (systems, points)
    return pl.pallas_call(
        kernel,
        name="gmres",
        out_shape=(field, field),
        in_specs=[smem] * 8 + [hbm] * 5,
        out_specs=(vmem, vmem),
        scratch_shapes=[
            pltpu.VMEM((systems, panels), F32),
            pltpu.VMEM((systems, panels), F32),
            pltpu.VMEM((systems, panels), F32),
            pltpu.VMEM(basis.shape, BF16),
            pltpu.VMEM(transfer.shape, BF16),
            pltpu.VMEM(basis.shape, BF16),
            pltpu.VMEM((parents * far_src.shape[1], coeffs, coeffs), BF16),
            pltpu.VMEM(near_blocks.shape, BF16),
            pltpu.VMEM((pairs, *cell), F32),
            pltpu.VMEM((clusters, *cell), F32),
            pltpu.VMEM((clusters, *cell), F32),
            pltpu.VMEM((slots + 8, *cell), F32),
            pltpu.VMEM((2, clusters, *cell), BF16),
            pltpu.VMEM((2, clusters, *cell), BF16),
            pltpu.VMEM((2, parents, *cell), BF16),
            pltpu.VMEM((2, slots, *cell), BF16),
            pltpu.VMEM((CHILDREN * parents, *cell), BF16),
            pltpu.VMEM((CHILDREN * parents, *cell), BF16),
            pltpu.VMEM((clusters, *cell), BF16),
            pltpu.VMEM((clusters, *cell), BF16),
            pltpu.VMEM((slots, *cell), BF16),
            pltpu.VMEM((slots, *cell), BF16),
            pltpu.VMEM((clusters, *cell), BF16),
            pltpu.VMEM((clusters, *cell), BF16),
            pltpu.VMEM((1, points), F32),
            pltpu.VMEM((devices, 1, points), F32),
            pltpu.SemaphoreType.DMA((19,)),
            pltpu.SemaphoreType.DMA((9, 2)),
        ],
        compiler_params=pltpu.CompilerParams(
            collective_id=0, has_side_effects=True, vmem_limit_bytes=60 << 20
        ),
    )(
        near_target,
        order.reshape(-1),
        far_src.reshape(-1),
        inverse,
        source,
        perm,
        keep,
        last,
        right_side,
        basis,
        transfer,
        far_mats.reshape(-1, coeffs, coeffs),
        near_blocks,
    )


def solution(mesh):
    placed = (
        P(None, AXES),
        P(AXES, None, None),
        P(AXES, None, None),
        P(AXES, None),
        P(AXES, None),
        P(AXES, None, None, None),
        P(AXES),
        P(AXES, None),
        P(AXES),
        P(AXES, None, None),
    )
    return jax.shard_map(
        local,
        mesh=mesh,
        in_specs=placed,
        out_specs=(P(None, AXES), P(None, AXES)),
        check_vma=False,
    )
```

time: 273 us -> 117 us (0.43)
  Pallas kernels: 0 us -> 83.9 us
  blocking collectives: 73 us -> 0 us
  starting transfers between devices: 58.5 us -> 11.5 us
  matrix products: 45.6 us -> 0 us
  waiting for transfers between devices: 47.3 us -> 7.13 us
  local copies, waits for them, and re-layouts: 38.8 us -> 6.47 us
    pallas_call x0 -> x1, Pallas kernels: none -> 83.9 us  [local(): pl.pallas_call(kernel, name='gmres', out_shape=(field, field), in_specs=[...]
    all_gather x3 -> x0, blocking collectives: 73 us -> none  [the longest x1 53 us: local(): dots = jnp.sum(lax.all_gather(own, ('leaf', 'level')), axis=0)]
    all_to_all x7 -> x1, starting transfers between devices: 58.5 us -> 11.5 us  [local(): lax.all_to_all(label.reshape(devices, CAPACITY), AXES, split_axis=0, conc...]
    dot_general x10 -> x0, matrix products: 45.6 us -> none  [the longest x2 13.9 us: operator(): jnp.einsum('srk,spk->rsp', expanded, basis_slot, preferred_element_type=j...]
    all_to_all x7 -> x1, waiting for transfers between devices: 47.3 us -> 7.13 us  [local(): lax.all_to_all(label.reshape(devices, CAPACITY), AXES, split_axis=0, conc...]
    gather x12 -> x0, local copies, waits for them, and re-layouts: 16.9 us -> none  [the longest x1 5.24 us: local(): transfer_slot = jnp.take(transfer, permutation, axis=0)]
    scatter x4 -> x0, local copies, waits for them, and re-layouts: 16.4 us -> none  [the longest x2 14.1 us: near_field(): outgoing = jnp.zeros((groups * capacity, systems, points), jnp.float32).a...]
    unnamed x17 -> x3, local copies, waits for them, and re-layouts: 0.23 us -> 4.5 us
  transfers between devices with their start and end apart: 7 -> 1, of which waited for: 4 -> 1; matrix products, arithmetic and copies ran while one was open for 19% -> 2% of each run, Pallas kernels for 0% -> 0%
where the time goes in v2:
time: 117 us
  Pallas kernels  83.9 us (72%)
  starting transfers between devices  11.5 us (10%)
  other arithmetic  7.17 us (6%)
  waiting for transfers between devices  7.13 us (6%)
  local copies, waits for them, and re-layouts  6.47 us (6%)
    pallas_call x1, Pallas kernels, local(): pl.pallas_call(kernel, name='gmres', out_shape=(field, field), in_specs=[...  83.9 us
    all_to_all x1, starting transfers between devices, local(): lax.all_to_all(label.reshape(devices, CAPACITY), AXES, split_axis=0, conc...  11.5 us
    all_to_all x1, waiting for transfers between devices, local(): lax.all_to_all(label.reshape(devices, CAPACITY), AXES, split_axis=0, conc...  7.13 us
    unnamed x3, local copies, waits for them, and re-layouts  4.5 us
  transfers between devices with their start and end apart: 1, of which 1 were waited for; matrix products, arithmetic and copies ran while one was open for 2% of the time, Pallas kernels for 0%

profile of v2, /device:TPU:1, one launch (start us, length us, event | category | flops | bytes accessed | tf_op | source)
XLA Modules:
  0.0 116.8 jit_solution(2674683410697885114)
XLA Ops:
  0.6 0.9 convert_reduce_fusion.4
  1.6 0.7 multiply_add_fusion
  2.3 0.8 select_reduce_fusion.2
  3.1 0.7 add.37
  3.8 11.5 %all-to-all-start = ((s32[128,1,4]{2,1,0:T(1,128)}), s32[128,1,4]{2,1,0:T(1,128)S(1)}, u32[]{:S(2)}, u32[]{:S(2)}) async-start(s32[128,1,4]{2,1,0:T(1,128)} %bitcast.2), calls=%async_computation | async-start | bytes 131072 | tf_op jit(solution)/shard_map/all_to_all | solution.py:359
  15.3 1.3 %select_reduce_fusion.4.inverse_ref = s32[128]{0:T(128)} fusion(s32[128]{0:T(128)} %bitcast.7), kind=kLoop, calls=%fused_computation.17 | loop fusion | flops 49024 | bytes 1024 | tf_op jit(solution)/shard_map/reduce_sum | solution.py:350
  16.6 0.8 copy.16
  17.4 0.6 reshape.51.far_ref
  18.0 7.1 %all-to-all-done = s32[128,1,4]{2,1,0:T(1,128)S(1)} async-done(((s32[128,1,4]{2,1,0:T(1,128)}), s32[128,1,4]{2,1,0:T(1,128)S(1)}, u32[]{:S(2)}, u32[]{:S(2)}) %all-to-all-start) | async-done | bytes 2080 | tf_op jit(solution)/shard_map/all_to_all | solution.py:359
  25.2 0.5 broadcast.49
  25.7 0.8 reduce.3
  26.5 0.1 lt.48
  26.6 0.1 convert_reduce_fusion.2
  26.7 0.3 convert_reduce_fusion
  27.1 0.9 select_reduce_fusion
  28.0 0.6 fusion.2.keep_ref
  28.6 0.6 compare_select_fusion.last_ref
  29.2 83.9 %gmres.1 = (f32[8,16384]{1,0:T(8,128)}, f32[8,16384]{1,0:T(8,128)}) custom-call(s32[256]{0:T(256)} %target_ref.1, s32[128]{0:T(128)} %bitcast.8, s32[128]{0:T(128)} %reshape.51.far_ref, s32[128]{0:T(128)} %select_reduce_fusion.4.inverse_ref, s32[512]{0:T(512)} %get-tuple-element.9.source_ref, s32[512]{0:T(512)} %get-tuple-element.5.perm_ref, ...), custom_call_target="tpu_custom_call" | custom-call | tf_op jit(solution)/shard_map/gmres/pallas_call | solution.py:378
  113.1 1.9 %copy.20 = f32[8,16384]{1,0:T(8,128)} copy(f32[8,16384]{1,0:T(8,128)} %get-tuple-element.14) | data formatting | bytes 1048576
  114.9 1.9 %copy.21 = f32[8,16384]{1,0:T(8,128)} copy(f32[8,16384]{1,0:T(8,128)} %get-tuple-element.15) | data formatting | bytes 1048576
  (2 shorter events, 0.0 us)
Async XLA Ops:
  3.8 21.3 %all-to-all-start = ((s32[128,1,4]{2,1,0:T(1,128)}), s32[128,1,4]{2,1,0:T(1,128)S(1)}, u32[]{:S(2)}, u32[]{:S(2)}) async-start(s32[128,1,4]{2,1,0:T(1,128)} %bitcast.2), calls=%async_computation | async-start | bytes 131072 | tf_op jit(solution)/shard_map/all_to_all | solution.py:359

commit v3 on v2

v3 whole, which is shorter than its diff:
```python
import functools

import jax
import jax.numpy as jnp
from jax import lax
from jax.experimental import pallas as pl
from jax.experimental.pallas import tpu as pltpu
from jax.sharding import PartitionSpec as P

CHILDREN = 4
CAPACITY = 4
EPSILON = 1e-06
SCALE = 2.0**-20
STRIDE = 37
AXES = ("leaf", "level")
LOGICAL = pl.DeviceIdType.LOGICAL
F32 = jnp.float32
BF16 = jnp.bfloat16


def combine(dots):
    start_sq = dots[0] + EPSILON
    start_norm = jnp.sqrt(start_sq)
    xx, xzs, zzs, xu, zu, uu = (dots[k] / start_sq for k in range(6))
    xz = xzs / SCALE
    zz = zzs / (SCALE * SCALE)
    along_one = 0.5 * xx + xz
    kappa = along_one - 0.5
    rest_raw = zz - 2.0 * kappa * xz + kappa * kappa * xx
    rest_sq = rest_raw + EPSILON
    rest_one = jnp.sqrt(rest_sq)
    scaled_rest = SCALE * rest_one
    scaled_sq = scaled_rest * scaled_rest
    beta = (xz - kappa * xx) / rest_one
    gamma = rest_raw / rest_sq
    one_t = (xu - kappa * xzs) / scaled_rest
    two_t = (zu - kappa * zzs - SCALE * kappa * (xu - kappa * xzs)) / scaled_sq
    t_t = (uu - 2.0 * kappa * zu + kappa * kappa * zzs) / scaled_sq
    cross_two = 0.5 * beta + one_t
    along_two = 0.5 * gamma + two_t
    short = 0.5 - along_two
    tail_sq = (
        t_t
        + short * short * gamma
        + cross_two * cross_two * xx
        + 2.0 * short * two_t
        - 2.0 * cross_two * one_t
        - 2.0 * cross_two * short * beta
    )
    gram_first = along_one * along_one + rest_one * rest_one
    gram_cross = along_one * cross_two + rest_one * along_two
    gram_last = cross_two * cross_two + along_two * along_two + tail_sq
    determinant = gram_first * gram_last - gram_cross * gram_cross
    coef_one = start_norm * (along_one * gram_last - cross_two * gram_cross) / determinant
    coef_two = start_norm * (gram_first * cross_two - gram_cross * along_one) / determinant
    one = coef_one / start_norm
    two = coef_two / (start_norm * rest_one)
    scaled_two = coef_two / (start_norm * scaled_rest)
    return (
        one - kappa * two,
        scaled_two,
        1.0 - 0.5 * one + 0.5 * kappa * two,
        -one / SCALE - (0.5 - kappa) * scaled_two,
        -scaled_two,
    )


def loop(count, unroll, body):
    def step(block, carry):
        for u in range(unroll):
            body(block * unroll + u)
        return carry

    lax.fori_loop(0, count // unroll, step, 0)


def send_tables(dest, source, order, slots, labels):
    size = order.shape[1]
    lane = lax.broadcasted_iota(jnp.int32, (size, size), 1)
    row = lax.broadcasted_iota(jnp.int32, (size, size), 0)

    def upright(values):
        return jnp.sum(jnp.where(lane == row, values, 0), axis=1, keepdims=True)

    halves = dest.shape[0]
    dest_row = [dest[h : h + 1, :] for h in range(halves)]
    dest_col = [upright(values) for values in dest_row]
    source_col = [upright(source[h : h + 1, :]) for h in range(halves)]
    rank = []
    for h in range(halves):
        total = jnp.zeros((size, 1), jnp.int32)
        for g in range(h + 1):
            same = dest_col[h] == dest_row[g]
            if g == h:
                same = same & (lane < row)
            total = total + jnp.sum(jnp.where(same, 1, 0), axis=1, keepdims=True)
        rank.append(total)
    every = []
    for k in range(CAPACITY):
        pair = jnp.zeros((1, size), jnp.int32)
        label = jnp.full((1, size), size, jnp.int32)
        for h in range(halves):
            chosen = (dest_col[h] == lane) & (rank[h] == k)
            pair = pair + jnp.sum(jnp.where(chosen, row + h * size, 0), axis=0, keepdims=True)
            label = label + jnp.sum(
                jnp.where(chosen, source_col[h] - size, 0), axis=0, keepdims=True
            )
        slots[pl.ds(k, 1), :] = pair
        every.append(label)
    inverse = jnp.sum(jnp.where(upright(order) == lane, row, 0), axis=0, keepdims=True)
    slots[pl.ds(CAPACITY, 1), :] = jnp.minimum(inverse, size - 1)
    mixed = jnp.zeros((size, size), jnp.int32)
    for k in range(CAPACITY):
        mixed = jnp.where(lane == k, upright(every[k]), mixed)
    labels[...] = mixed.astype(F32).reshape(labels.shape)


def land_tables(labels, out):
    size = labels.shape[0]
    lane = lax.broadcasted_iota(jnp.int32, (size, size), 1)
    row = lax.broadcasted_iota(jnp.int32, (size, size), 0)
    columns = [labels[:, k : k + 1] for k in range(CAPACITY)]
    rows = [
        jnp.sum(jnp.where(lane == row, columns[k], 0), axis=0, keepdims=True)
        for k in range(CAPACITY)
    ]
    upto = jnp.zeros((size, size), jnp.int32)
    some = jnp.zeros((size, size), jnp.int32)
    perm = [jnp.zeros((size, size), jnp.int32) for _ in range(CAPACITY)]
    first = [jnp.zeros((size, size), jnp.int32) for _ in range(CAPACITY)]
    for k in range(CAPACITY):
        less = jnp.zeros((size, size), jnp.int32)
        tied = jnp.zeros((size, size), jnp.int32)
        for j in range(CAPACITY):
            less = less + jnp.where(rows[j] < columns[k], 1, 0)
            if j < k:
                tied = tied + jnp.where(rows[j] == columns[k], 1, 0)
            elif j == k:
                tied = tied + jnp.where((rows[j] == columns[k]) & (lane < row), 1, 0)
        below = jnp.sum(less, axis=1, keepdims=True)
        place = below + jnp.sum(tied, axis=1, keepdims=True)
        upto = upto + jnp.where(columns[k] <= lane, 1, 0)
        some = some + jnp.where(columns[k] == lane, 1, 0)
        for b in range(CAPACITY):
            here = place == lane + b * size
            perm[b] = perm[b] + jnp.where(here, CAPACITY * row + k, 0)
            first[b] = first[b] + jnp.where(here, below, 0)
    for b in range(CAPACITY):
        out[pl.ds(b, 1), :] = jnp.sum(perm[b], axis=0, keepdims=True)
        start = jnp.sum(first[b], axis=0, keepdims=True)
        out[pl.ds(CAPACITY + b, 1), :] = jnp.where(start == lane[0:1] + b * size, 0, 1)
    ends = jnp.sum(upto, axis=0, keepdims=True) - 1
    out[pl.ds(2 * CAPACITY, 1), :] = jnp.where(
        jnp.sum(some, axis=0, keepdims=True) > 0, ends, CAPACITY * size
    )


def kernel(
    target_ref, order_ref, far_ref,
    dest_ref, source_ref, order_row,
    x_hbm, basis_hbm, transfer_hbm, far_hbm, near_hbm,
    z_ref, u_ref, coef_ref,
    x_ref, basis_ref, transfer_ref, product_ref, turned_ref, far_w, near_w,
    part_ref, field_ref, run_ref,
    up_send, up_recv, down_send, near_send,
    table_one, table_two, down_one, down_two, near_one, near_two, cast_one, cast_two,
    dot_send, dot_recv, label_send, label_recv,
    slot_rows, land_rows, slot_of, land_of,
    load_sem, table_sem, remote_sem,
):
    clusters = basis_ref.shape[0]
    devices = clusters
    levels = lax.axis_size("level")
    leaf, level = lax.axis_index("leaf"), lax.axis_index("level")
    leaves = devices // levels
    me = leaf * levels + level
    pairs = near_w.shape[0]
    parents = clusters // CHILDREN
    partners = far_w.shape[0] // parents
    lanes = basis_ref.shape[1]
    systems = x_ref.shape[0]
    chunks = 8
    rows = clusters // chunks

    load_x = pltpu.make_async_copy(x_hbm, x_ref, load_sem.at[0])
    loads = []
    for k in range(chunks):
        part = pl.ds(k * rows, rows)
        loads.append(
            pltpu.make_async_copy(basis_hbm.at[part], basis_ref.at[part], load_sem.at[1 + 2 * k])
        )
        loads.append(
            pltpu.make_async_copy(
                transfer_hbm.at[part], transfer_ref.at[part], load_sem.at[2 + 2 * k]
            )
        )
    load_near = pltpu.make_async_copy(near_hbm, near_w, load_sem.at[1 + 2 * chunks])
    load_far = pltpu.make_async_copy(far_hbm, far_w, load_sem.at[2 + 2 * chunks])
    load_x.start()
    for copy in loads:
        copy.start()
    load_near.start()
    load_far.start()

    def peer(i):
        return (me + STRIDE * i) % devices

    barrier = pltpu.get_barrier_semaphore()

    def greet(i, carry):
        pl.semaphore_signal(barrier, inc=1, device_id=peer(i), device_id_type=LOGICAL)
        return carry

    lax.fori_loop(1, devices, greet, 0, unroll=8)

    def push(src, dst, stage, device):
        pltpu.make_async_remote_copy(
            src_ref=src,
            dst_ref=dst,
            send_sem=remote_sem.at[stage, 0],
            recv_sem=remote_sem.at[stage, 1],
            device_id=device,
            device_id_type=LOGICAL,
        ).start()

    def settle(ref, stage):
        for end in range(2):
            pltpu.make_async_copy(ref, ref, remote_sem.at[stage, end]).wait()

    def push_all(lo, hi, stage, src, dst):
        def go(i, carry):
            other = peer(i)
            push(src(other), dst, stage, other)
            return carry

        lax.fori_loop(lo, hi, go, 0, unroll=8)

    def tile(ref, c):
        return ref[:, pl.ds(pl.multiple_of(c * lanes, lanes), lanes)]

    send_tables(dest_ref[...], source_ref[...], order_row[...], slot_rows, label_send)
    move_slots = pltpu.make_async_copy(slot_rows, slot_of, table_sem.at[0])
    move_slots.start()
    run_ref[CAPACITY * devices] = jnp.zeros(run_ref.shape[1:], F32)
    load_x.wait()

    def cast(c):
        cast_one[c] = tile(x_ref, c).astype(BF16)

    loop(clusters, 16, cast)
    for k in range(chunks):
        loads[2 * k].wait()
        loads[2 * k + 1].wait()

        def fuse(c, k=k):
            product_ref[k * rows + c] = jnp.dot(
                basis_ref[k * rows + c], transfer_ref[k * rows + c], preferred_element_type=F32
            ).astype(BF16)

        loop(rows, 8, fuse)
    move_slots.wait()
    pl.semaphore_wait(barrier, devices - 1)

    zero = jnp.zeros((systems, lanes), F32)
    dots = []
    for trip in range(2):
        first = trip == 0
        stage = 4 * trip
        table_ref = table_one if first else table_two
        down_recv = down_one if first else down_two
        near_recv = near_one if first else near_two
        cast_ref = cast_one if first else cast_two

        def lift(s):
            c = order_ref[s]
            return jnp.dot(cast_ref[c], product_ref[c], preferred_element_type=F32).astype(BF16)

        def up(i, carry):
            other = peer(i)
            up_send[trip, other] = lift(other)
            push(up_send.at[trip, other], up_recv.at[trip, me], stage, other)
            return carry

        lax.fori_loop(1, devices, up, 0, unroll=8)
        up_recv[trip, me] = lift(me)

        if first:
            load_near.wait()

        def near_product(n):
            part_ref[n] = jnp.dot(
                cast_ref[target_ref[n]], near_w[n], preferred_element_type=F32
            )

        loop(pairs, 32, near_product)

        def place(d):
            for k in range(CAPACITY):
                near_send[trip, CAPACITY * d + k] = part_ref[slot_of[k, d]].astype(BF16)

        loop(devices, 4, place)
        for k in range(CAPACITY):
            near_recv[CAPACITY * me + k] = part_ref[slot_of[k, me]].astype(BF16)

        def near_push(lo, hi):
            push_all(
                lo,
                hi,
                stage + 3,
                lambda e: near_send.at[trip, pl.ds(CAPACITY * e, CAPACITY)],
                near_recv.at[pl.ds(CAPACITY * me, CAPACITY)],
            )

        near_push(1, 43)
        if first:
            label_recv[pl.ds(me, 1)] = label_send[pl.ds(me, 1)]
            push_all(1, devices, 9, lambda e: label_send.at[e], label_recv.at[me])
        settle(up_recv.at[trip, pl.ds(0, devices - 1)], stage)

        def gather_parent(q):
            total = up_recv[trip, CHILDREN * q].astype(F32)
            for i in range(1, CHILDREN):
                total = total + up_recv[trip, CHILDREN * q + i].astype(F32)
            table_ref[level * parents + q] = total.astype(BF16)

        loop(parents, 8, gather_parent)
        mine = table_ref.at[pl.ds(level * parents, parents)]
        for i in range(1, CHILDREN):
            push(mine, mine, stage + 1, leaf * levels + (level + i) % levels)
        near_push(43, 85)
        if first:

            def turn(c):
                turned_ref[c] = product_ref[c].T

            loop(clusters, 8, turn)
            load_far.wait()
        settle(table_ref.at[pl.ds(0, (levels - 1) * parents)], stage + 1)

        def translate(q):
            picked = jnp.concatenate(
                [table_ref[far_ref[k, q]] for k in range(partners)], axis=1
            )
            mats = far_w[pl.ds(partners * q, partners)].reshape(partners * lanes, lanes)
            return jnp.dot(picked, mats, preferred_element_type=F32).astype(BF16)

        def down(q, skip):
            value = translate(q)
            down_send[trip, q] = value
            for i in range(skip, levels):
                push(
                    down_send.at[trip, q],
                    down_recv.at[me],
                    stage + 2,
                    q * levels + (level + i) % levels,
                )
            return value

        down_recv[me] = down(leaf, 1)

        def down_step(j, carry):
            down((leaf + 13 * j) % leaves, 0)
            return carry

        lax.fori_loop(1, leaves, down_step, 0, unroll=4)
        near_push(85, devices)
        if first:
            settle(label_recv.at[pl.ds(0, devices - 1)], 9)
            land_tables(
                label_recv[...].reshape(devices, lanes).astype(jnp.int32), land_rows
            )
            move_land = pltpu.make_async_copy(land_rows, land_of, table_sem.at[1])
            move_land.start()
            move_land.wait()
        settle(down_recv.at[pl.ds(0, devices - 1)], stage + 2)

        def spread(c):
            field_ref[c] = jnp.dot(
                down_recv[slot_of[CAPACITY, c]], turned_ref[c], preferred_element_type=F32
            )

        loop(clusters, 32, spread)
        settle(near_recv.at[pl.ds(0, CAPACITY * (devices - 1))], stage + 3)

        for b in range(CAPACITY):

            def land(block, total):
                for u in range(8):
                    i = block * 8 + u
                    total = total * land_of[CAPACITY + b, i].astype(F32) + near_recv[
                        land_of[b, i]
                    ].astype(F32)
                    run_ref[b * devices + i] = total
                return total

            total = lax.fori_loop(0, devices // 8, land, zero if b == 0 else total)

        def finish(block, sums):
            sums = list(sums)
            for u in range(8):
                c = block * 8 + u
                where = pl.ds(pl.multiple_of(c * lanes, lanes), lanes)
                value = field_ref[c] + run_ref[land_of[2 * CAPACITY, c]]
                x = x_ref[:, where]
                if first:
                    value = value * SCALE
                    z_ref[:, where] = value
                    cast_two[c] = value.astype(BF16)
                    terms = ((x, x), (x, value), (value, value))
                else:
                    u_ref[:, where] = value
                    terms = ((x, value), (z_ref[:, where], value), (value, value))
                for k, (p, q) in enumerate(terms):
                    sums[k] = sums[k] + p * q
            return tuple(sums)

        dots += lax.fori_loop(0, clusters // 8, finish, (zero,) * 3)

    lane = lax.broadcasted_iota(jnp.int32, (systems, lanes), 1)
    row = lax.broadcasted_iota(jnp.int32, (systems, lanes), 0)
    packed = zero
    for k, total in enumerate(dots):
        packed = jnp.where(
            lane == row + k * systems, jnp.sum(total, axis=1, keepdims=True), packed
        )
    packed = jnp.sum(packed, axis=0, keepdims=True)
    dot_send[...] = packed
    dot_recv[pl.ds(me, 1)] = packed[None]
    push_all(1, devices, 8, lambda e: dot_send, dot_recv.at[me])
    settle(dot_recv.at[pl.ds(0, devices - 1)], 8)
    gathered = jnp.broadcast_to(jnp.sum(dot_recv[...], axis=0), (systems, lanes))
    scalars = combine(
        [
            jnp.sum(jnp.where(lane == row + k * systems, gathered, 0.0), axis=1, keepdims=True)
            for k in range(len(dots))
        ]
    )
    for k, value in enumerate(scalars):
        coef_ref[k] = jnp.broadcast_to(value, (systems, lanes))


def local(
    right_side,
    basis,
    transfer,
    order,
    far_src,
    far_mats,
    near_target,
    near_dest,
    near_src,
    near_blocks,
):
    systems, panels = right_side.shape
    clusters, points, coeffs = basis.shape
    devices = lax.axis_size(AXES)
    pairs = near_target.shape[0]
    parents = clusters // CHILDREN
    slots = CAPACITY * devices
    smem = pl.BlockSpec(memory_space=pltpu.SMEM)
    hbm = pl.BlockSpec(memory_space=pl.ANY)
    vmem = pl.BlockSpec(memory_space=pltpu.VMEM)
    field = jax.ShapeDtypeStruct((systems, panels), F32)
    cell = (systems, points)
    image, second, coefs = pl.pallas_call(
        kernel,
        name="gmres",
        out_shape=(field, field, jax.ShapeDtypeStruct((5, systems, points), F32)),
        in_specs=[smem] * 3 + [vmem] * 3 + [hbm] * 5,
        out_specs=(vmem, vmem, vmem),
        scratch_shapes=[
            pltpu.VMEM((systems, panels), F32),
            pltpu.VMEM(basis.shape, BF16),
            pltpu.VMEM(transfer.shape, BF16),
            pltpu.VMEM(basis.shape, BF16),
            pltpu.VMEM(basis.shape, BF16),
            pltpu.VMEM((parents * far_src.shape[1], coeffs, coeffs), BF16),
            pltpu.VMEM(near_blocks.shape, BF16),
            pltpu.VMEM((pairs, *cell), F32),
            pltpu.VMEM((clusters, *cell), F32),
            pltpu.VMEM((slots + 8, *cell), F32),
            pltpu.VMEM((2, clusters, *cell), BF16),
            pltpu.VMEM((2, clusters, *cell), BF16),
            pltpu.VMEM((2, parents, *cell), BF16),
            pltpu.VMEM((2, slots, *cell), BF16),
            pltpu.VMEM((CHILDREN * parents, *cell), BF16),
            pltpu.VMEM((CHILDREN * parents, *cell), BF16),
            pltpu.VMEM((clusters, *cell), BF16),
            pltpu.VMEM((clusters, *cell), BF16),
            pltpu.VMEM((slots, *cell), BF16),
            pltpu.VMEM((slots, *cell), BF16),
            pltpu.VMEM((clusters, *cell), BF16),
            pltpu.VMEM((clusters, *cell), BF16),
            pltpu.VMEM((1, points), F32),
            pltpu.VMEM((devices, 1, points), F32),
            pltpu.VMEM((devices, 1, points), F32),
            pltpu.VMEM((devices, 1, points), F32),
            pltpu.VMEM((8, devices), jnp.int32),
            pltpu.VMEM((16, devices), jnp.int32),
            pltpu.SMEM((8, devices), jnp.int32),
            pltpu.SMEM((16, devices), jnp.int32),
            pltpu.SemaphoreType.DMA((19,)),
            pltpu.SemaphoreType.DMA((2,)),
            pltpu.SemaphoreType.DMA((10, 2)),
        ],
        compiler_params=pltpu.CompilerParams(
            collective_id=0, has_side_effects=True, vmem_limit_bytes=60 << 20
        ),
    )(
        near_target,
        order.reshape(-1),
        far_src.T,
        near_dest.reshape(-1, points),
        near_src.reshape(-1, points),
        order,
        right_side,
        basis,
        transfer,
        far_mats.reshape(-1, coeffs, coeffs),
        near_blocks,
    )
    first_x, first_z, second_x, second_z, second_u = (coefs[k, :, :1] for k in range(5))
    return (
        first_x * right_side + first_z * image,
        second_x * right_side + second_z * image + second_u * second,
    )


def solution(mesh):
    placed = (
        P(None, AXES),
        P(AXES, None, None),
        P(AXES, None, None),
        P(AXES, None),
        P(AXES, None),
        P(AXES, None, None, None),
        P(AXES),
        P(AXES, None),
        P(AXES),
        P(AXES, None, None),
    )
    return jax.shard_map(
        local,
        mesh=mesh,
        in_specs=placed,
        out_specs=(P(None, AXES), P(None, AXES)),
        check_vma=False,
    )
```

time: 117 us -> 122 us (1.043)
  Pallas kernels: 83.9 us -> 118 us
  starting transfers between devices: 11.5 us -> 0 us
  waiting for transfers between devices: 7.13 us -> 0 us
  local copies, waits for them, and re-layouts: 6.47 us -> 0.88 us
  other arithmetic: 7.17 us -> 2.38 us
    pallas_call x1, Pallas kernels: 83.9 us -> 118 us  [local(): pl.pallas_call(kernel, name='gmres', out_shape=(field, field, jax.ShapeDt...]
    all_to_all x1 -> x0, starting transfers between devices: 11.5 us -> none  [local(): lax.all_to_all(label.reshape(devices, CAPACITY), AXES, split_axis=0, conc...]
    all_to_all x1 -> x0, waiting for transfers between devices: 7.13 us -> none  [local(): lax.all_to_all(label.reshape(devices, CAPACITY), AXES, split_axis=0, conc...]
    unnamed x3 -> x2, local copies, waits for them, and re-layouts: 4.5 us -> 0.01 us
    reduce_sum x6 -> x0, other arithmetic: 4.48 us -> none  [the longest x1 1.31 us: local(): jnp.sum(ints(order[0][None, :] == index[:, None]) * index[None, :], axis=1)]
    add x3 -> x1, other arithmetic: 0.72 us -> 2.38 us  [local(): second_x * right_side + second_z * image + second_u * second]
  transfers between devices with their start and end apart: 1 -> 0, of which waited for: 1 -> 0; matrix products, arithmetic and copies ran while one was open for 2% -> 0% of each run, Pallas kernels for 0% -> 0%
where the time goes in v3:
time: 122 us
  Pallas kernels  118 us (97%)
  other arithmetic  2.38 us (2%)
    pallas_call x1, Pallas kernels, local(): pl.pallas_call(kernel, name='gmres', out_shape=(field, field, jax.ShapeDt...  118 us

profile of v3, /device:TPU:1, one launch (start us, length us, event | category | flops | bytes accessed | tf_op | source)
XLA Modules:
  0.0 122.3 jit_solution(7985964292247256409)
XLA Ops:
  0.6 0.0 copy-start
  0.6 118.3 %gmres.1 = (f32[8,16384]{1,0:T(8,128)}, f32[8,16384]{1,0:T(8,128)}, f32[5,8,128]{2,1,0:T(8,128)}) custom-call(s32[256]{0:T(256)} %target_ref.1, s32[128]{0:T(128)} %bitcast.6, s32[4,32]{1,0:T(4,128)} %bitcast.7, s32[2,128]{1,0:T(2,128)} %bitcast.8, s32[2,128]{1,0:T(2,128)} %bitcast.9, s32[1,128]{1,0:T(1,128)} %order_row.1, f32[8,16384]{1,0:T(8,128)} %x_hbm.1, ...), custom_call_target="tpu_custom_call" | custom-call | tf_op jit(solution)/shard_map/gmres/pallas_call | solution.py:465
  119.0 0.9 slice_reduce_fusion.2
  119.9 0.0 copy-done
  119.9 2.4 %multiply_add_fusion = (f32[8,16384]{1,0:T(8,128)}, f32[8,16384]{1,0:T(8,128)}) fusion(f32[8,16384]{1,0:T(8,128)} %get-tuple-element.7, f32[8,16384]{1,0:T(8,128)} %get-tuple-element.6, f32[8,16384]{1,0:T(8,128)S(1)} %copy-done, f32[8]{0:T(128)S(1)} %get-tuple-element.9, f32[8]{0:T(128)S(1)} %get-tuple-element.10, f32[8]{0:T(128)S(1)} %get-tuple-element.8, ...), kind=kLoop, calls=%fused_computation | loop fusion | flops 1048576 | bytes 2621600 | tf_op jit(solution)/shard_map/add | solution.py:525
Async XLA Ops:
  0.6 119.2 %copy-start = (f32[8,16384]{1,0:T(8,128)S(1)}, f32[8,16384]{1,0:T(8,128)}, u32[]{:S(2)}) copy-start(f32[8,16384]{1,0:T(8,128)} %x_hbm.1) | copy-start | bytes 1572868

commit v4 on v3

--- a/solution.py
+++ b/solution.py
@@ -12,6 +12,10 @@
 EPSILON = 1e-06
 SCALE = 2.0**-20
 STRIDE = 37
+BLOCK = 16
+GREET = 18
+SPLIT = 96
+TEAM = 16
 AXES = ("leaf", "level")
 LOGICAL = pl.DeviceIdType.LOGICAL
 F32 = jnp.float32
@@ -74,7 +78,7 @@
     lax.fori_loop(0, count // unroll, step, 0)
 
 
-def send_tables(dest, source, order, slots, labels):
+def send_tables(me, greet, dest, source, order, slots, labels):
     size = order.shape[1]
     lane = lax.broadcasted_iota(jnp.int32, (size, size), 1)
     row = lax.broadcasted_iota(jnp.int32, (size, size), 0)
@@ -86,29 +90,51 @@
     dest_row = [dest[h : h + 1, :] for h in range(halves)]
     dest_col = [upright(values) for values in dest_row]
     source_col = [upright(source[h : h + 1, :]) for h in range(halves)]
+
+    def turn_of(group):
+        return ((group - me + size) * pow(STRIDE, -1, size) + size - 1) % size
+
+    turn_row = [turn_of(values) for values in dest_row]
+    turn_col = [turn_of(values) for values in dest_col]
+    greet()
     rank = []
+    place = []
     for h in range(halves):
         total = jnp.zeros((size, 1), jnp.int32)
-        for g in range(h + 1):
+        count = jnp.zeros((size, size), jnp.int32)
+        for g in range(halves):
+            count = count + jnp.where(turn_row[g] < turn_col[h], 1, 0)
+            if g > h:
+                continue
             same = dest_col[h] == dest_row[g]
             if g == h:
                 same = same & (lane < row)
             total = total + jnp.sum(jnp.where(same, 1, 0), axis=1, keepdims=True)
         rank.append(total)
+        greet()
+        place.append(total + jnp.sum(count, axis=1, keepdims=True))
     every = []
     for k in range(CAPACITY):
         pair = jnp.zeros((1, size), jnp.int32)
         label = jnp.full((1, size), size, jnp.int32)
         for h in range(halves):
             chosen = (dest_col[h] == lane) & (rank[h] == k)
-            pair = pair + jnp.sum(jnp.where(chosen, row + h * size, 0), axis=0, keepdims=True)
+            pair = pair + jnp.sum(jnp.where(chosen, place[h], 0), axis=0, keepdims=True)
             label = label + jnp.sum(
                 jnp.where(chosen, source_col[h] - size, 0), axis=0, keepdims=True
             )
         slots[pl.ds(k, 1), :] = pair
         every.append(label)
+        greet()
     inverse = jnp.sum(jnp.where(upright(order) == lane, row, 0), axis=0, keepdims=True)
     slots[pl.ds(CAPACITY, 1), :] = jnp.minimum(inverse, size - 1)
+    for b in range(halves):
+        pair = jnp.zeros((1, size), jnp.int32)
+        for h in range(halves):
+            pair = pair + jnp.sum(
+                jnp.where(place[h] == lane + b * size, row + h * size, 0), axis=0, keepdims=True
+            )
+        slots[pl.ds(CAPACITY + 1 + b, 1), :] = pair
     mixed = jnp.zeros((size, size), jnp.int32)
     for k in range(CAPACITY):
         mixed = jnp.where(lane == k, upright(every[k]), mixed)
@@ -161,7 +187,7 @@
     x_hbm, basis_hbm, transfer_hbm, far_hbm, near_hbm,
     z_ref, u_ref, coef_ref,
     x_ref, basis_ref, transfer_ref, product_ref, turned_ref, far_w, near_w,
-    part_ref, field_ref, run_ref,
+    part_ref, field_ref, run_ref, expansion_ref,
     up_send, up_recv, down_send, near_send,
     table_one, table_two, down_one, down_two, near_one, near_two, cast_one, cast_two,
     dot_send, dot_recv, label_send, label_recv,
@@ -179,25 +205,24 @@
     partners = far_w.shape[0] // parents
     lanes = basis_ref.shape[1]
     systems = x_ref.shape[0]
-    chunks = 8
+    chunks = 4
     rows = clusters // chunks
 
     load_x = pltpu.make_async_copy(x_hbm, x_ref, load_sem.at[0])
-    loads = []
-    for k in range(chunks):
-        part = pl.ds(k * rows, rows)
-        loads.append(
-            pltpu.make_async_copy(basis_hbm.at[part], basis_ref.at[part], load_sem.at[1 + 2 * k])
-        )
-        loads.append(
+    def parts(src, dst, base):
+        return [
             pltpu.make_async_copy(
-                transfer_hbm.at[part], transfer_ref.at[part], load_sem.at[2 + 2 * k]
+                src.at[pl.ds(k * rows, rows)], dst.at[pl.ds(k * rows, rows)], load_sem.at[base + k]
             )
-        )
+            for k in range(chunks)
+        ]
+
+    load_basis = parts(basis_hbm, basis_ref, 1)
+    load_transfer = parts(transfer_hbm, transfer_ref, 1 + chunks)
     load_near = pltpu.make_async_copy(near_hbm, near_w, load_sem.at[1 + 2 * chunks])
     load_far = pltpu.make_async_copy(far_hbm, far_w, load_sem.at[2 + 2 * chunks])
     load_x.start()
-    for copy in loads:
+    for copy in load_basis + load_transfer:
         copy.start()
     load_near.start()
     load_far.start()
@@ -207,11 +232,12 @@
 
     barrier = pltpu.get_barrier_semaphore()
 
-    def greet(i, carry):
-        pl.semaphore_signal(barrier, inc=1, device_id=peer(i), device_id_type=LOGICAL)
-        return carry
-
-    lax.fori_loop(1, devices, greet, 0, unroll=8)
+    greeted = [1]
+
+    def greet():
+        for i in range(greeted[0], min(greeted[0] + GREET, devices)):
+            pl.semaphore_signal(barrier, inc=1, device_id=peer(i), device_id_type=LOGICAL)
+        greeted[0] = min(greeted[0] + GREET, devices)
 
     def push(src, dst, stage, device):
         pltpu.make_async_remote_copy(
@@ -223,9 +249,11 @@
             device_id_type=LOGICAL,
         ).start()
 
+    sent = []
+
     def settle(ref, stage):
-        for end in range(2):
-            pltpu.make_async_copy(ref, ref, remote_sem.at[stage, end]).wait()
+        pltpu.make_async_copy(ref, ref, remote_sem.at[stage, 1]).wait()
+        sent.append(pltpu.make_async_copy(ref, ref, remote_sem.at[stage, 0]))
 
     def push_all(lo, hi, stage, src, dst):
         def go(i, carry):
@@ -238,27 +266,28 @@
     def tile(ref, c):
         return ref[:, pl.ds(pl.multiple_of(c * lanes, lanes), lanes)]
 
-    send_tables(dest_ref[...], source_ref[...], order_row[...], slot_rows, label_send)
+    send_tables(
+        me, greet, dest_ref[...], source_ref[...], order_row[...], slot_rows, label_send
+    )
+    while greeted[0] < devices:
+        greet()
     move_slots = pltpu.make_async_copy(slot_rows, slot_of, table_sem.at[0])
     move_slots.start()
     run_ref[CAPACITY * devices] = jnp.zeros(run_ref.shape[1:], F32)
     load_x.wait()
-
-    def cast(c):
-        cast_one[c] = tile(x_ref, c).astype(BF16)
-
-    loop(clusters, 16, cast)
     for k in range(chunks):
-        loads[2 * k].wait()
-        loads[2 * k + 1].wait()
-
-        def fuse(c, k=k):
-            product_ref[k * rows + c] = jnp.dot(
-                basis_ref[k * rows + c], transfer_ref[k * rows + c], preferred_element_type=F32
+        load_basis[k].wait()
+
+        def expand(c, k=k):
+            value = tile(x_ref, k * rows + c).astype(BF16)
+            cast_one[k * rows + c] = value
+            expansion_ref[k * rows + c] = jnp.dot(
+                value, basis_ref[k * rows + c], preferred_element_type=F32
             ).astype(BF16)
 
-        loop(rows, 8, fuse)
-    move_slots.wait()
+        loop(rows, 32, expand)
+    for copy in load_transfer:
+        copy.wait()
     pl.semaphore_wait(barrier, devices - 1)
 
     zero = jnp.zeros((systems, lanes), F32)
@@ -271,38 +300,64 @@
         near_recv = near_one if first else near_two
         cast_ref = cast_one if first else cast_two
 
-        def lift(s):
-            c = order_ref[s]
-            return jnp.dot(cast_ref[c], product_ref[c], preferred_element_type=F32).astype(BF16)
-
-        def up(i, carry):
-            other = peer(i)
-            up_send[trip, other] = lift(other)
-            push(up_send.at[trip, other], up_recv.at[trip, me], stage, other)
+        before, matrix = (expansion_ref, transfer_ref) if first else (cast_two, product_ref)
+
+        def lift(block):
+            values = []
+            for u in range(BLOCK):
+                c = order_ref[peer(1 + block * BLOCK + u)]
+                values.append(
+                    jnp.dot(before[c], matrix[c], preferred_element_type=F32).astype(BF16)
+                )
+            return values
+
+        def hold(block, values):
+            for u in range(BLOCK):
+                up_send[trip, peer(1 + block * BLOCK + u)] = values[u]
+
+        def send_up(block, count):
+            for u in range(count):
+                other = peer(1 + block * BLOCK + u)
+                push(up_send.at[trip, other], up_recv.at[trip, me], stage, other)
+
+        hold(0, lift(0))
+
+        def up(block, carry):
+            values = lift(block)
+            send_up(block - 1, BLOCK)
+            hold(block, values)
             return carry
 
-        lax.fori_loop(1, devices, up, 0, unroll=8)
-        up_recv[trip, me] = lift(me)
+        blocks = devices // BLOCK
+        lax.fori_loop(1, blocks, up, 0)
+        send_up(blocks - 1, BLOCK - 1)
+        up_recv[trip, me] = up_send[trip, me]
 
         if first:
             load_near.wait()
 
-        def near_product(n):
-            part_ref[n] = jnp.dot(
-                cast_ref[target_ref[n]], near_w[n], preferred_element_type=F32
-            )
-
-        loop(pairs, 32, near_product)
-
-        def place(d):
-            for k in range(CAPACITY):
-                near_send[trip, CAPACITY * d + k] = part_ref[slot_of[k, d]].astype(BF16)
-
-        loop(devices, 4, place)
-        for k in range(CAPACITY):
-            near_recv[CAPACITY * me + k] = part_ref[slot_of[k, me]].astype(BF16)
+        if first:
+            move_slots.wait()
+
+        piece = pairs // CAPACITY
+
+        def near_product(b):
+            def one(j):
+                n = slot_of[CAPACITY + 1 + b * piece // lanes, b * piece % lanes + j]
+                part_ref[b * piece + j] = jnp.dot(
+                    cast_ref[target_ref[n]], near_w[n], preferred_element_type=F32
+                )
+
+            loop(piece, 32, one)
 
         def near_push(lo, hi):
+            def fill(i, carry):
+                d = peer(i)
+                for k in range(CAPACITY):
+                    near_send[trip, CAPACITY * d + k] = part_ref[slot_of[k, d]].astype(BF16)
+                return carry
+
+            lax.fori_loop(lo, hi, fill, 0, unroll=4)
             push_all(
                 lo,
                 hi,
@@ -311,10 +366,10 @@
                 near_recv.at[pl.ds(CAPACITY * me, CAPACITY)],
             )
 
-        near_push(1, 43)
-        if first:
-            label_recv[pl.ds(me, 1)] = label_send[pl.ds(me, 1)]
-            push_all(1, devices, 9, lambda e: label_send.at[e], label_recv.at[me])
+        step = piece // CAPACITY
+        near_product(0)
+        near_product(1)
+        near_push(1, 1 + 2 * step)
         settle(up_recv.at[trip, pl.ds(0, devices - 1)], stage)
 
         def gather_parent(q):
@@ -327,43 +382,65 @@
         mine = table_ref.at[pl.ds(level * parents, parents)]
         for i in range(1, CHILDREN):
             push(mine, mine, stage + 1, leaf * levels + (level + i) % levels)
-        near_push(43, 85)
+        near_product(2)
+        near_product(3)
+        near_push(1 + 2 * step, SPLIT)
         if first:
-
-            def turn(c):
-                turned_ref[c] = product_ref[c].T
-
-            loop(clusters, 8, turn)
+            label_recv[pl.ds(me, 1)] = label_send[pl.ds(me, 1)]
+            push_all(1, devices, 9, lambda e: label_send.at[e], label_recv.at[me])
+
+            def fuse(c):
+                value = jnp.dot(
+                    basis_ref[c], transfer_ref[c], preferred_element_type=F32
+                ).astype(BF16)
+                product_ref[c] = value
+                turned_ref[c] = value.T
+
+            loop(clusters, 8, fuse)
             load_far.wait()
         settle(table_ref.at[pl.ds(0, (levels - 1) * parents)], stage + 1)
 
-        def translate(q):
-            picked = jnp.concatenate(
-                [table_ref[far_ref[k, q]] for k in range(partners)], axis=1
-            )
-            mats = far_w[pl.ds(partners * q, partners)].reshape(partners * lanes, lanes)
-            return jnp.dot(picked, mats, preferred_element_type=F32).astype(BF16)
-
-        def down(q, skip):
-            value = translate(q)
-            down_send[trip, q] = value
-            for i in range(skip, levels):
-                push(
-                    down_send.at[trip, q],
-                    down_recv.at[me],
-                    stage + 2,
-                    q * levels + (level + i) % levels,
+        def parent_of(j):
+            return (leaf + 13 * j) % leaves
+
+        group = BLOCK // levels
+
+        def translate(block):
+            values = []
+            for u in range(group):
+                q = parent_of(1 + block * group + u)
+                picked = jnp.concatenate(
+                    [table_ref[far_ref[k, q]] for k in range(partners)], axis=1
                 )
-            return value
-
-        down_recv[me] = down(leaf, 1)
-
-        def down_step(j, carry):
-            down((leaf + 13 * j) % leaves, 0)
+                mats = far_w[pl.ds(partners * q, partners)].reshape(partners * lanes, lanes)
+                values.append(jnp.dot(picked, mats, preferred_element_type=F32).astype(BF16))
+            return values
+
+        def keep(block, values):
+            for u in range(group):
+                down_send[trip, parent_of(1 + block * group + u)] = values[u]
+
+        def send_down(block, last):
+            for u in range(group):
+                q = parent_of(1 + block * group + u)
+                for i in range(1 if last and u == group - 1 else 0, levels):
+                    other = q * levels + (level + i) % levels
+                    push(down_send.at[trip, q], down_recv.at[me], stage + 2, other)
+
+        keep(0, translate(0))
+
+        def down(block, carry):
+            values = translate(block)
+            send_down(block - 1, False)
+            keep(block, values)
             return carry
 
-        lax.fori_loop(1, leaves, down_step, 0, unroll=4)
-        near_push(85, devices)
+        lax.fori_loop(1, blocks, down, 0)
+        send_down(blocks - 1, True)
+        down_recv[me] = down_send[trip, leaf]
+        near_push(SPLIT, devices)
+        for k in range(CAPACITY):
+            near_recv[CAPACITY * me + k] = part_ref[slot_of[k, me]].astype(BF16)
         if first:
             settle(label_recv.at[pl.ds(0, devices - 1)], 9)
             land_tables(
@@ -424,11 +501,21 @@
             lane == row + k * systems, jnp.sum(total, axis=1, keepdims=True), packed
         )
     packed = jnp.sum(packed, axis=0, keepdims=True)
-    dot_send[...] = packed
-    dot_recv[pl.ds(me, 1)] = packed[None]
-    push_all(1, devices, 8, lambda e: dot_send, dot_recv.at[me])
-    settle(dot_recv.at[pl.ds(0, devices - 1)], 8)
-    gathered = jnp.broadcast_to(jnp.sum(dot_recv[...], axis=0), (systems, lanes))
+    teams = devices // TEAM
+    team, member = me // TEAM, me % TEAM
+    dot_send[0] = packed
+    dot_recv[pl.ds(member, 1)] = packed[None]
+    for i in range(1, TEAM):
+        push(dot_send.at[0], dot_recv.at[member], 8, team * TEAM + (member + i) % TEAM)
+    settle(dot_recv.at[pl.ds(0, TEAM - 1)], 8)
+    packed = jnp.sum(dot_recv[pl.ds(0, TEAM)], axis=0)
+    dot_send[1] = packed
+    dot_recv[pl.ds(TEAM + team, 1)] = packed[None]
+    for i in range(1, teams):
+        push(dot_send.at[1], dot_recv.at[TEAM + team], 10, (me + TEAM * i) % devices)
+    settle(dot_recv.at[pl.ds(TEAM, teams - 1)], 10)
+    packed = jnp.sum(dot_recv[pl.ds(TEAM, teams)], axis=0)
+    gathered = jnp.broadcast_to(packed, (systems, lanes))
     scalars = combine(
         [
             jnp.sum(jnp.where(lane == row + k * systems, gathered, 0.0), axis=1, keepdims=True)
@@ -437,6 +524,18 @@
     )
     for k, value in enumerate(scalars):
         coef_ref[k] = jnp.broadcast_to(value, (systems, lanes))
+    for copy in sent:
+        copy.wait()
+
+
+def finish(coef_ref, x_ref, z_ref, u_ref, solved_ref, left_ref):
+    first_x, first_z, second_x, second_z, second_u = (coef_ref[k] for k in range(5))
+    lanes = coef_ref.shape[2]
+    for c in range(x_ref.shape[1] // lanes):
+        where = pl.ds(c * lanes, lanes)
+        x, z, u = x_ref[:, where], z_ref[:, where], u_ref[:, where]
+        solved_ref[:, where] = first_x * x + first_z * z
+        left_ref[:, where] = second_x * x + second_z * z + second_u * u
 
 
 def local(
@@ -458,7 +557,7 @@
     parents = clusters // CHILDREN
     slots = CAPACITY * devices
     smem = pl.BlockSpec(memory_space=pltpu.SMEM)
-    hbm = pl.BlockSpec(memory_space=pl.ANY)
+    hbm = pl.BlockSpec(memory_space=pltpu.HBM)
     vmem = pl.BlockSpec(memory_space=pltpu.VMEM)
     field = jax.ShapeDtypeStruct((systems, panels), F32)
     cell = (systems, points)
@@ -479,6 +578,7 @@
             pltpu.VMEM((pairs, *cell), F32),
             pltpu.VMEM((clusters, *cell), F32),
             pltpu.VMEM((slots + 8, *cell), F32),
+            pltpu.VMEM((clusters, *cell), BF16),
             pltpu.VMEM((2, clusters, *cell), BF16),
             pltpu.VMEM((2, clusters, *cell), BF16),
             pltpu.VMEM((2, parents, *cell), BF16),
@@ -491,17 +591,17 @@
             pltpu.VMEM((slots, *cell), BF16),
             pltpu.VMEM((clusters, *cell), BF16),
             pltpu.VMEM((clusters, *cell), BF16),
-            pltpu.VMEM((1, points), F32),
-            pltpu.VMEM((devices, 1, points), F32),
+            pltpu.VMEM((2, 1, points), F32),
+            pltpu.VMEM((TEAM + devices // TEAM, 1, points), F32),
             pltpu.VMEM((devices, 1, points), F32),
             pltpu.VMEM((devices, 1, points), F32),
             pltpu.VMEM((8, devices), jnp.int32),
             pltpu.VMEM((16, devices), jnp.int32),
             pltpu.SMEM((8, devices), jnp.int32),
             pltpu.SMEM((16, devices), jnp.int32),
-            pltpu.SemaphoreType.DMA((19,)),
+            pltpu.SemaphoreType.DMA((11,)),
             pltpu.SemaphoreType.DMA((2,)),
-            pltpu.SemaphoreType.DMA((10, 2)),
+            pltpu.SemaphoreType.DMA((11, 2)),
         ],
         compiler_params=pltpu.CompilerParams(
             collective_id=0, has_side_effects=True, vmem_limit_bytes=60 << 20
@@ -519,11 +619,16 @@
         far_mats.reshape(-1, coeffs, coeffs),
         near_blocks,
     )
-    first_x, first_z, second_x, second_z, second_u = (coefs[k, :, :1] for k in range(5))
-    return (
-        first_x * right_side + first_z * image,
-        second_x * right_side + second_z * image + second_u * second,
-    )
+    block = pl.BlockSpec((systems, panels // 4), lambda i: (0, i))
+    return pl.pallas_call(
+        finish,
+        name="outputs",
+        grid=(4,),
+        out_shape=(field, field),
+        in_specs=[pl.BlockSpec((5, systems, points), lambda i: (0, 0, 0))] + [block] * 3,
+        out_specs=(block, block),
+        compiler_params=pltpu.CompilerParams(vmem_limit_bytes=60 << 20),
+    )(coefs, right_side, image, second)
 
 
 def solution(mesh):

time: 122 us -> 85.9 us (0.70)
  Pallas kernels: 118 us -> 84.9 us
  other arithmetic: 2.38 us -> 0 us
    pallas_call x1, Pallas kernels: 118 us -> 81.4 us  [local(): pl.pallas_call(kernel, name='gmres', out_shape=(field, field, jax.ShapeDt...]
    pallas_call x0 -> x1, Pallas kernels: none -> 3.56 us  [local(): pl.pallas_call(finish, name='outputs', grid=(4,), out_shape=(field, field...]
    add x1 -> x0, other arithmetic: 2.38 us -> none  [local(): second_x * right_side + second_z * image + second_u * second]
where the time goes in v4:
time: 85.9 us; the launch traced here: 85.6 us
  Pallas kernels  84.9 us (99%)
    pallas_call x1, Pallas kernels, local(): pl.pallas_call(kernel, name='gmres', out_shape=(field, field, jax.ShapeDt...  81.4 us
    pallas_call x1, Pallas kernels, local(): pl.pallas_call(finish, name='outputs', grid=(4,), out_shape=(field, field...  3.56 us

profile of v4, /device:TPU:1, one launch (start us, length us, event | category | flops | bytes accessed | tf_op | source)
XLA Modules:
  0.0 85.6 jit_solution(14663318136503546518)
XLA Ops:
  0.6 81.4 %gmres.1 = (f32[8,16384]{1,0:T(8,128)}, f32[8,16384]{1,0:T(8,128)}, f32[5,8,128]{2,1,0:T(8,128)}) custom-call(s32[256]{0:T(256)} %target_ref.1, s32[128]{0:T(128)} %bitcast.6, s32[4,32]{1,0:T(4,128)} %bitcast.7, s32[2,128]{1,0:T(2,128)} %bitcast.8, s32[2,128]{1,0:T(2,128)} %bitcast.9, s32[1,128]{1,0:T(1,128)} %order_row.1, f32[8,16384]{1,0:T(8,128)} %x_ref.1, ...), custom_call_target="tpu_custom_call" | custom-call | tf_op jit(solution)/shard_map/gmres/pallas_call | solution.py:564
  82.0 3.6 %outputs.1 = (f32[8,16384]{1,0:T(8,128)}, f32[8,16384]{1,0:T(8,128)}) custom-call(f32[5,8,128]{2,1,0:T(8,128)} %get-tuple-element.5.coef_ref, f32[8,16384]{1,0:T(8,128)} %x_ref.1, f32[8,16384]{1,0:T(8,128)} %get-tuple-element.6.z_ref, f32[8,16384]{1,0:T(8,128)} %get-tuple-element.7.u_ref), custom_call_target="tpu_custom_call" | custom-call | tf_op jit(solution)/shard_map/outputs/pallas_call | solution.py:623

commit v5 on v4

--- a/solution.py
+++ b/solution.py
@@ -185,8 +185,8 @@
     target_ref, order_ref, far_ref,
     dest_ref, source_ref, order_row,
     x_hbm, basis_hbm, transfer_hbm, far_hbm, near_hbm,
-    z_ref, u_ref, coef_ref,
-    x_ref, basis_ref, transfer_ref, product_ref, turned_ref, far_w, near_w,
+    z_hbm, u_hbm, coef_ref,
+    z_ref, u_ref, x_ref, basis_ref, transfer_ref, product_ref, turned_ref, far_w, near_w,
     part_ref, field_ref, run_ref, expansion_ref,
     up_send, up_recv, down_send, near_send,
     table_one, table_two, down_one, down_two, near_one, near_two, cast_one, cast_two,
@@ -288,6 +288,18 @@
         loop(rows, 32, expand)
     for copy in load_transfer:
         copy.wait()
+    piece = pairs // CAPACITY
+
+    def near_product(field, b):
+        def one(j):
+            n = slot_of[CAPACITY + 1 + b * piece // lanes, b * piece % lanes + j]
+            part_ref[b * piece + j] = jnp.dot(
+                field[target_ref[n]], near_w[n], preferred_element_type=F32
+            )
+
+        loop(piece, 32, one)
+
+    move_slots.wait()
     pl.semaphore_wait(barrier, devices - 1)
 
     zero = jnp.zeros((systems, lanes), F32)
@@ -332,23 +344,8 @@
         lax.fori_loop(1, blocks, up, 0)
         send_up(blocks - 1, BLOCK - 1)
         up_recv[trip, me] = up_send[trip, me]
-
         if first:
             load_near.wait()
-
-        if first:
-            move_slots.wait()
-
-        piece = pairs // CAPACITY
-
-        def near_product(b):
-            def one(j):
-                n = slot_of[CAPACITY + 1 + b * piece // lanes, b * piece % lanes + j]
-                part_ref[b * piece + j] = jnp.dot(
-                    cast_ref[target_ref[n]], near_w[n], preferred_element_type=F32
-                )
-
-            loop(piece, 32, one)
 
         def near_push(lo, hi):
             def fill(i, carry):
@@ -367,8 +364,8 @@
             )
 
         step = piece // CAPACITY
-        near_product(0)
-        near_product(1)
+        for b in range(2):
+            near_product(cast_ref, b)
         near_push(1, 1 + 2 * step)
         settle(up_recv.at[trip, pl.ds(0, devices - 1)], stage)
 
@@ -382,8 +379,8 @@
         mine = table_ref.at[pl.ds(level * parents, parents)]
         for i in range(1, CHILDREN):
             push(mine, mine, stage + 1, leaf * levels + (level + i) % levels)
-        near_product(2)
-        near_product(3)
+        for b in range(2, CAPACITY):
+            near_product(cast_ref, b)
         near_push(1 + 2 * step, SPLIT)
         if first:
             label_recv[pl.ds(me, 1)] = label_send[pl.ds(me, 1)]
@@ -492,6 +489,11 @@
             return tuple(sums)
 
         dots += lax.fori_loop(0, clusters // 8, finish, (zero,) * 3)
+        store = pltpu.make_async_copy(
+            z_ref if first else u_ref, z_hbm if first else u_hbm, table_sem.at[2 + trip]
+        )
+        store.start()
+        sent.append(store)
 
     lane = lax.broadcasted_iota(jnp.int32, (systems, lanes), 1)
     row = lax.broadcasted_iota(jnp.int32, (systems, lanes), 0)
@@ -566,8 +568,10 @@
         name="gmres",
         out_shape=(field, field, jax.ShapeDtypeStruct((5, systems, points), F32)),
         in_specs=[smem] * 3 + [vmem] * 3 + [hbm] * 5,
-        out_specs=(vmem, vmem, vmem),
+        out_specs=(hbm, hbm, vmem),
         scratch_shapes=[
+            pltpu.VMEM((systems, panels), F32),
+            pltpu.VMEM((systems, panels), F32),
             pltpu.VMEM((systems, panels), F32),
             pltpu.VMEM(basis.shape, BF16),
             pltpu.VMEM(transfer.shape, BF16),
@@ -600,7 +604,7 @@
             pltpu.SMEM((8, devices), jnp.int32),
             pltpu.SMEM((16, devices), jnp.int32),
             pltpu.SemaphoreType.DMA((11,)),
-            pltpu.SemaphoreType.DMA((2,)),
+            pltpu.SemaphoreType.DMA((4,)),
             pltpu.SemaphoreType.DMA((11, 2)),
         ],
         compiler_params=pltpu.CompilerParams(
@@ -619,11 +623,11 @@
         far_mats.reshape(-1, coeffs, coeffs),
         near_blocks,
     )
-    block = pl.BlockSpec((systems, panels // 4), lambda i: (0, i))
+    block = pl.BlockSpec((systems, panels // 2), lambda i: (0, i))
     return pl.pallas_call(
         finish,
         name="outputs",
-        grid=(4,),
+        grid=(2,),
         out_shape=(field, field),
         in_specs=[pl.BlockSpec((5, systems, points), lambda i: (0, 0, 0))] + [block] * 3,
         out_specs=(block, block),

time: 85.9 us -> 84.2 us (0.980)
  Pallas kernels: 84.9 us -> 83.3 us
    pallas_call x1, Pallas kernels: 3.56 us -> 2.25 us  [local(): pl.pallas_call(finish, name='outputs', grid=(2,), out_shape=(field, field...]
where the time goes in v5:
time: 84.2 us; the launch traced here: 84 us
  Pallas kernels  83.3 us (99%)
    pallas_call x1, Pallas kernels, local(): pl.pallas_call(kernel, name='gmres', out_shape=(field, field, jax.ShapeDt...  81.1 us
    pallas_call x1, Pallas kernels, local(): pl.pallas_call(finish, name='outputs', grid=(2,), out_shape=(field, field...  2.25 us

profile of v5, /device:TPU:1, one launch (start us, length us, event | category | flops | bytes accessed | tf_op | source)
XLA Modules:
  0.0 84.0 jit_solution(1568074948875998652)
XLA Ops:
  0.6 81.1 %gmres.1 = (f32[8,16384]{1,0:T(8,128)}, f32[8,16384]{1,0:T(8,128)}, f32[5,8,128]{2,1,0:T(8,128)}) custom-call(s32[256]{0:T(256)} %target_ref.1, s32[128]{0:T(128)} %bitcast.6, s32[4,32]{1,0:T(4,128)} %bitcast.7, s32[2,128]{1,0:T(2,128)} %bitcast.8, s32[2,128]{1,0:T(2,128)} %bitcast.9, s32[1,128]{1,0:T(1,128)} %order_row.1, f32[8,16384]{1,0:T(8,128)} %x_ref.1, ...), custom_call_target="tpu_custom_call" | custom-call | tf_op jit(solution)/shard_map/gmres/pallas_call | solution.py:566
  81.7 2.2 %outputs.1 = (f32[8,16384]{1,0:T(8,128)}, f32[8,16384]{1,0:T(8,128)}) custom-call(f32[5,8,128]{2,1,0:T(8,128)} %get-tuple-element.5.coef_ref, f32[8,16384]{1,0:T(8,128)} %x_ref.1, f32[8,16384]{1,0:T(8,128)} %get-tuple-element.6.z_ref, f32[8,16384]{1,0:T(8,128)} %get-tuple-element.7.u_ref), custom_call_target="tpu_custom_call" | custom-call | tf_op jit(solution)/shard_map/outputs/pallas_call | solution.py:627

commit v6 on v5

--- a/solution.py
+++ b/solution.py
@@ -12,7 +12,7 @@
 EPSILON = 1e-06
 SCALE = 2.0**-20
 STRIDE = 37
-BLOCK = 16
+BLOCK = 32
 GREET = 18
 SPLIT = 96
 TEAM = 16

time: 84.2 us -> 84.1 us (level)
  no operation moved by 1% of the time
where the time goes in v6:
time: 84.1 us; the launch traced here: 83.6 us
  Pallas kernels  83 us (99%)
    pallas_call x1, Pallas kernels, local(): pl.pallas_call(kernel, name='gmres', out_shape=(field, field, jax.ShapeDt...  80.7 us
    pallas_call x1, Pallas kernels, local(): pl.pallas_call(finish, name='outputs', grid=(2,), out_shape=(field, field...  2.25 us

profile of v6, /device:TPU:1, one launch (start us, length us, event | category | flops | bytes accessed | tf_op | source)
XLA Modules:
  0.0 83.6 jit_solution(7364202876385727166)
XLA Ops:
  0.6 80.7 %gmres.1 = (f32[8,16384]{1,0:T(8,128)}, f32[8,16384]{1,0:T(8,128)}, f32[5,8,128]{2,1,0:T(8,128)}) custom-call(s32[256]{0:T(256)} %target_ref.1, s32[128]{0:T(128)} %bitcast.6, s32[4,32]{1,0:T(4,128)} %bitcast.7, s32[2,128]{1,0:T(2,128)} %bitcast.8, s32[2,128]{1,0:T(2,128)} %bitcast.9, s32[1,128]{1,0:T(1,128)} %order_row.1, f32[8,16384]{1,0:T(8,128)} %x_ref.1, ...), custom_call_target="tpu_custom_call" | custom-call | tf_op jit(solution)/shard_map/gmres/pallas_call | solution.py:566
  81.4 2.2 %outputs.1 = (f32[8,16384]{1,0:T(8,128)}, f32[8,16384]{1,0:T(8,128)}) custom-call(f32[5,8,128]{2,1,0:T(8,128)} %get-tuple-element.5.coef_ref, f32[8,16384]{1,0:T(8,128)} %x_ref.1, f32[8,16384]{1,0:T(8,128)} %get-tuple-element.6.z_ref, f32[8,16384]{1,0:T(8,128)} %get-tuple-element.7.u_ref), custom_call_target="tpu_custom_call" | custom-call | tf_op jit(solution)/shard_map/outputs/pallas_call | solution.py:627
